TPU v7x, 128 devices: a whole 4x4x4 slice. The times are simulated.
128 devices in a mesh: ens: 8 (over y_lo, z), rep: 16 (over y_hi, x, core).
Axes of the slice: x: 4, y: 4 (y_hi: 2, y_lo: 2; y = y_hi * 2 + y_lo), z: 4, core: 2. Of those that a mesh axis runs over, the one named last changes fastest.
Arguments:
- cur_states: bfloat16 [32768, 4096], P('rep'), may hold values from -6 to 6
- buffer: bfloat16 [4096, 4096], P('rep'), may hold values from -6 to 6
- fetch_rows: int32 [16, 16, 128], P('rep'), may hold values from 0 to 255
- fetch_counts: int32 [16, 16], replicated, may hold values from 1 to 128, as said below
- actions: int32 [32768], P('rep'), may hold values from 0 to 255
- rewards: float32 [32768], P('rep'), may hold values from -0.5 to 0.5
- terminal: int32 [32768], P('rep'), may hold values 0 or 1
- mc_return: float32 [32768], P('rep'), may hold values from 0 to 1
- w_in: bfloat16 [8, 4096, 512], P('ens'), may hold values from -0.09375 to 0.09375
- w_out: bfloat16 [8, 512, 256], P('ens'), may hold values from -0.25 to 0.25
Outputs:
- targets: float32 [32768], P('rep')
- grad_in: float32 [8, 4096, 512], P('ens', 'rep')
- grad_out: float32 [8, 512, 256], P('ens', 'rep')
Inputs may be any that keep to these rules, and one draw needn't show every extreme that they name: `fetch_rows`: each entry indexes the owner's own rows. `fetch_counts`: entry [o, r] is how many leading slots of requester r at owner o are used; some entry equals 128 in every draw.
All inputs are finite; a program needn't handle non-finite values. No bound on the sum of `terminal` on one device may be relied on, other than what follows from the above.
Results may differ from a plain program's by a relative error of at most 0.0044.
Values may be sent and summed in bfloat16 or wider, within the bound.
No kernel may reach another device: no remote copies, remote signals or barrier semaphores. Data moves between devices by JAX's collectives and lax.ppermute only.
A program may use at most 192 MiB of HBM per device.

v0:
```python
import functools

import jax
import jax.numpy as jnp
from jax import lax
from jax.experimental import pallas as pl
from jax.experimental.pallas import tpu as pltpu
from jax.sharding import PartitionSpec as P


UNIT = 16
BLOCK = 256
F32, BF16 = jnp.float32, jnp.bfloat16
VMEM = pl.BlockSpec(memory_space=pltpu.VMEM)
SMEM = pl.BlockSpec(memory_space=pltpu.SMEM)
HBM = pl.BlockSpec(memory_space=pltpu.HBM)


def place(y, x, core):
    return y * 8 + x * 2 + core


def moves(fn):
    return [
        (place(y, x, c), place(*fn(y, x, c)))
        for y in range(2)
        for x in range(4)
        for c in range(2)
    ]


CORE = moves(lambda y, x, c: (y, x, 1 - c))
RIGHT = moves(lambda y, x, c: (y, (x + 1) % 4, c))
LEFT = moves(lambda y, x, c: (y, (x + 3) % 4, c))
ACROSS = moves(lambda y, x, c: (1 - y, x, c))


def sent(value, pairs):
    return lax.ppermute(value, "rep", pairs)


def low(value):
    return value.astype(BF16)


def high(value):
    return value.astype(F32)


def after(value, *others):
    return lax.optimization_barrier((value, *others))


def call(
    kernel, out_shape, in_specs, scratch=(), out_specs=None, limit=16, flops=0,
    bytes_moved=1 << 20,
):
    single = not isinstance(out_shape, (list, tuple))
    if out_specs is None:
        out_specs = VMEM if single else [VMEM] * len(out_shape)
    return pl.pallas_call(
        kernel,
        out_shape=out_shape,
        in_specs=in_specs,
        out_specs=out_specs,
        scratch_shapes=list(scratch),
        compiler_params=pltpu.CompilerParams(vmem_limit_bytes=limit << 20),
        cost_estimate=pl.CostEstimate(
            flops=flops, bytes_accessed=bytes_moved, transcendentals=0
        ),
    )


def in_hbm(array):
    return pltpu.with_memory_space_constraint(array, pltpu.HBM)


def shape(dims, dtype=F32):
    return jax.ShapeDtypeStruct(dims, dtype)


def units_of(count):
    return (count + (UNIT - 1)) >> 4


def gathered(counts_ref, states_ref, packed_ref, sem_at):
    me = lax.axis_index("rep")
    owners = counts_ref.shape[0]
    runs = states_ref.shape[0] // owners // UNIT

    def start(source, position):
        pltpu.make_async_copy(
            states_ref.at[pl.ds(pl.multiple_of(source * UNIT, UNIT), UNIT)],
            packed_ref.at[pl.ds(pl.multiple_of(position * UNIT, UNIT), UNIT)],
            sem_at(position >> 4),
        ).start()

    def owner(o, position):
        def unit(u, position):
            start(o * runs + u, position)
            return position + 1

        return lax.fori_loop(0, units_of(counts_ref[o, me]), unit, position)

    units = lax.fori_loop(0, owners, owner, jnp.int32(0))
    blocks = (units + (BLOCK // UNIT - 1)) >> 4
    lax.fori_loop(units, blocks * (BLOCK // UNIT), lambda p, c: (start(0, p), c)[1], 0)
    return blocks


def gathered_block(states_ref, packed_ref, sem):
    return pltpu.make_async_copy(states_ref.at[pl.ds(0, BLOCK)], packed_ref.at[pl.ds(0, BLOCK)], sem)


def pack_rows(counts_ref, values, packed_refs):
    me = lax.axis_index("rep")
    owners, cap = values[0].shape
    lane = lax.broadcasted_iota(jnp.int32, (1, cap), 1)
    for ref in packed_refs:
        ref[...] = jnp.zeros_like(ref)
    start = jnp.int32(0)
    for o in range(owners):
        count = counts_ref[o, me]
        row, shift = start >> 7, start & 127
        for value, ref in zip(values, packed_refs):
            kept = jnp.where(lane < count, value[o : o + 1, :], 0.0)
            turned = pltpu.roll(kept, shift, 1)
            ref[pl.ds(row, 1), :] += jnp.where(lane >= shift, turned, 0.0)
            ref[pl.ds(row + 1, 1), :] += jnp.where(lane < shift, turned, 0.0)
        start = start + units_of(count) * UNIT


def next_kernel(
    buffer_ref, w_in_ref, w_out_ref, fetch_ref, picked_ref, w_ref, rows_ref, w_second, fetch, total,
    found_rows, sems, small_sems,
):
    steps = sems.shape[1]
    depth = w_in_ref.shape[0] // steps
    copies = []
    for i in range(steps):
        part = pl.ds(i * depth, depth)
        pair = (
            pltpu.make_async_copy(w_in_ref.at[part], w_ref.at[part], sems.at[0, i]),
            pltpu.make_async_copy(buffer_ref.at[:, part], rows_ref.at[:, part], sems.at[1, i]),
        )
        for copy in pair:
            copy.start()
        copies.append(pair)
    second = pltpu.make_async_copy(w_out_ref, w_second, small_sems.at[0])
    wanted = pltpu.make_async_copy(fetch_ref, fetch, small_sems.at[1])
    second.start()
    wanted.start()
    for i in range(steps):
        for copy in copies[i]:
            copy.wait()
        part = pl.ds(i * depth, depth)
        term = jnp.dot(rows_ref[:, part], w_ref[part, :], preferred_element_type=F32)
        total[...] = term if i == 0 else total[...] + term
    preact = total[...]
    hidden = low(preact * jax.nn.sigmoid(preact))
    second.wait()
    wanted.wait()
    logits = jnp.dot(hidden, w_second[...], preferred_element_type=F32)
    best = jax.nn.sigmoid(jnp.max(logits, axis=1, keepdims=True))
    halves = [jnp.broadcast_to(best[i : i + 128], (128, 128)).T[:8] for i in (0, 128)]
    for i in range(0, fetch.shape[0], 8):
        rows = fetch[pl.ds(i, 8), :]
        found = [
            jnp.take_along_axis(half, rows & 127, axis=1, mode="promise_in_bounds")
            for half in halves
        ]
        picked = jnp.where(rows < 128, found[0], found[1])
        for d in range(found_rows.shape[0]):
            found_rows[d, pl.ds(i, 8), :] = picked
    out = pltpu.make_async_copy(found_rows, picked_ref, small_sems.at[2])
    out.start()
    out.wait()


def member_kernel(
    counts_ref, states_ref, w_first, w_second, table_ref, best_ref,
    actions_ref, rewards_ref, terminal_ref, returns_ref,
    targets_ref, packed_ref, d_hidden_ref, grad_ref, blocks_ref,
    preacts, target_row, scale_row, act_row, sems,
):
    me = lax.axis_index("rep")
    owners, cap = rewards_ref.shape
    blocks = gathered(counts_ref, states_ref, packed_ref, lambda b: sems.at[b])
    blocks_ref[...] = jnp.full(blocks_ref.shape, blocks, jnp.int32)
    counts = table_ref[...]
    counted = jnp.sum(counts).astype(F32)
    requester = lax.broadcasted_iota(jnp.int32, counts.shape, 1)
    mine = jnp.sum(jnp.where(requester == me, counts, 0), axis=1, keepdims=True)
    used = (lax.broadcasted_iota(jnp.int32, (owners, cap), 1) < mine).astype(F32)
    bootstrap = jnp.maximum(jnp.min(best_ref[...], axis=0), returns_ref[...])
    target = rewards_ref[...] + 0.98 * (1.0 - terminal_ref[...].astype(F32)) * bootstrap
    targets_ref[...] = used * target
    scale = used * 2.0 * (jnp.full((owners, cap), 65536.0, F32) / counted)
    pack_rows(
        counts_ref, [target, scale, high(actions_ref[...])], [target_row, scale_row, act_row]
    )
    grad_ref[...] = jnp.zeros_like(grad_ref)
    bins = lax.broadcasted_iota(jnp.int32, (grad_ref.shape[1], BLOCK), 0).astype(F32)
    w_out = w_second[...]
    w_out_turned = w_out.T

    def arrived(b):
        gathered_block(states_ref, packed_ref, sems.at[b]).wait()

    def begin(b):
        part = pl.ds(pl.multiple_of(b * BLOCK, BLOCK), BLOCK)
        preacts[b & 1] = jnp.dot(packed_ref[part, :], w_first[...], preferred_element_type=F32)

    def finish(b):
        at = pl.ds(pl.multiple_of(b * BLOCK, BLOCK), BLOCK)
        goal, scaled, acts = [
            jnp.concatenate([ref[pl.ds(2 * b + i, 1), :] for i in (0, 1)], axis=1)
            for ref in (target_row, scale_row, act_row)
        ]
        preact = preacts[b & 1].T
        sigmoid_pre = jax.nn.sigmoid(preact)
        hidden = low(preact * sigmoid_pre)
        logits = jnp.dot(w_out_turned, hidden, preferred_element_type=F32)
        chosen = bins == acts
        taken = jax.nn.sigmoid(jnp.sum(jnp.where(chosen, logits, 0.0), axis=0, keepdims=True))
        errors = (taken - goal) * taken * (1.0 - taken) * scaled
        d_logits = low(jnp.where(chosen, errors, 0.0))
        grad_ref[...] += lax.dot_general(
            hidden, d_logits, (((1,), (1,)), ((), ())), preferred_element_type=F32
        )
        back = jnp.dot(w_out, d_logits, preferred_element_type=F32)
        d_hidden_ref[:, at] = low(back * sigmoid_pre * (1.0 + preact * (1.0 - sigmoid_pre)))

    arrived(0)
    begin(jnp.int32(0))

    def step(b, carry):
        arrived(b)
        finish(b - 1)
        begin(b)
        return carry

    lax.fori_loop(1, blocks, step, 0)
    finish(blocks - 1)


def piece_kernel(steps, with_recv, stacked, blocks_ref, d_hidden_ref, states_ref, grad_ref, *rest):
    recv_ref = rest[0] if with_recv else None
    out_refs, total = rest[with_recv:-1], rest[-1]
    me = lax.axis_index("rep")
    y, x, core = me >> 3, (me >> 1) & 3, me & 1
    blocks = blocks_ref[0, 0]
    _, width, depth = total.shape
    rows = grad_ref.shape[0] // 16
    ats = [place(y ^ dy, (x + dx) & 3, core ^ dc) for dy, dx, dc in steps]

    for count in range(1, d_hidden_ref.shape[1] // BLOCK + 1):

        @pl.when(blocks == count)
        def _(deep=count * BLOCK):
            def piece(j, carry):
                at = ats[-1]
                for k in range(len(ats) - 1):
                    at = jnp.where(j == k, ats[k], at)
                columns = pl.ds(pl.multiple_of(at * depth, depth), depth)
                total[j] = jnp.dot(
                    d_hidden_ref[:, :deep], states_ref[:deep, columns], preferred_element_type=F32
                )
                return carry

            lax.fori_loop(0, len(ats), piece, 0)

    for j, at in enumerate(ats):
        first = total[j]
        second = grad_ref[pl.ds(pl.multiple_of(at * rows, rows), rows), :]
        if with_recv:
            first = first + high(recv_ref[j, pl.ds(0, width), :])
            second = second + high(recv_ref[j, pl.ds(width, rows), :])
        out = out_refs[0].at[j] if stacked else out_refs[j]
        out[pl.ds(0, width), :] = first.astype(out.dtype)
        out[pl.ds(width, rows), :] = second.astype(out.dtype)


def final_kernel(own_ref, left_ref, right_ref, over_ref, first_ref, second_ref):
    width = first_ref.shape[1]
    total = own_ref[...] + high(left_ref[...]) + high(right_ref[...]) + high(over_ref[...])
    first_ref[...] = total[:width].T
    second_ref[...] = total[width:]


def update(
    cur_states, buffer, fetch_rows, fetch_counts, actions, rewards, terminal, mc_return, w_in, w_out
):
    w_first, w_second = w_in[0], w_out[0]
    owners, cap = fetch_rows.shape[1:]
    slots, model = cur_states.shape
    width, bins = w_second.shape
    members = lax.axis_size("ens")
    grid = lambda a: a.reshape(owners, cap)

    picked, w_kept = call(
        next_kernel,
        [pltpu.HBM((members, owners, cap), F32), pltpu.VMEM(w_first.shape, BF16)],
        [HBM] * 4,
        [
            pltpu.VMEM(buffer.shape, BF16),
            pltpu.VMEM(w_second.shape, BF16),
            pltpu.VMEM((owners, cap), jnp.int32),
            pltpu.VMEM((buffer.shape[0], width), F32),
            pltpu.VMEM((members, owners, cap), F32),
            pltpu.SemaphoreType.DMA((2, 8)),
            pltpu.SemaphoreType.DMA((3,)),
        ],
        out_specs=[HBM, VMEM],
        flops=2 * buffer.shape[0] * model * width,
        bytes_moved=6 << 20,
    )(*[in_hbm(a) for a in (buffer, w_first, w_second, fetch_rows[0])])
    best = lax.all_to_all(
        picked.reshape(members * owners, 1, cap), ("ens", "rep"), 0, 0, tiled=True
    ).reshape(members, owners, cap)

    targets, packed, d_hidden, grad_second, blocks = call(
        member_kernel,
        [
            shape((owners, cap)),
            pltpu.VMEM((slots, model), BF16),
            pltpu.VMEM((width, slots), BF16),
            pltpu.VMEM((width, bins), F32),
            pltpu.VMEM((8, 128), jnp.int32),
        ],
        [SMEM, HBM] + [VMEM] * 8,
        [pltpu.VMEM((2, BLOCK, width), F32)]
        + [pltpu.VMEM((owners + 8, cap), F32)] * 3
        + [pltpu.SemaphoreType.DMA((slots // BLOCK,))],
        flops=slots * model * width,
        bytes_moved=14 << 20,
    )(
        fetch_counts, in_hbm(cur_states), w_kept, w_second, fetch_counts, best,
        grid(actions), grid(rewards), grid(terminal), grid(mc_return),
    )

    depth = model // 16
    tall = width + width // 16

    def pieces(source, steps, dtypes=None, recv=None):
        stacked = dtypes is None
        out = (
            shape((len(steps), tall, depth), BF16)
            if stacked
            else [shape((tall, depth), t) for t in dtypes]
        )
        extra = () if recv is None else (recv,)
        return call(
            functools.partial(piece_kernel, steps, len(extra), stacked),
            out,
            [VMEM] * (4 + len(extra)),
            [pltpu.VMEM((len(steps), width, depth), F32)],
            flops=len(steps) * slots * width * depth,
            bytes_moved=len(steps) << 18,
        )(blocks, source, packed, grad_second, *extra)

    far = [(1, 2), (0, 2)]
    near = [(1, 1), (1, 3), (0, 1), (0, 3)]
    own = [(1, 0), (0, 0)]
    theirs = lambda group: tuple((*g, 1) for g in group)
    ours = lambda group: tuple((*g, 0) for g in group)

    away_far = sent(pieces(d_hidden, theirs(far)), CORE)
    away_near = sent(pieces(d_hidden, theirs(near)), CORE)
    far_other, far_same = pieces(d_hidden, ours(far), (BF16, BF16), away_far)
    from_left_far = sent(far_other, RIGHT)
    from_right_far = sent(far_same, LEFT)
    away_own = sent(pieces(d_hidden, theirs(own)), CORE)
    right_other, left_other, right_same, left_same = pieces(
        d_hidden, ours(near), (F32, BF16, BF16, F32), away_near
    )
    from_right_other = sent(left_other, LEFT)
    own_other, own_same = pieces(d_hidden, ours(own), (F32, F32), away_own)
    right_other, left_same, own_same = after(right_other, left_same, own_same)
    from_left_other = sent(low(right_other + high(from_left_far)), RIGHT)
    from_right_same = sent(low(left_same + high(from_right_far)), LEFT)
    from_left_same = sent(right_same, RIGHT)
    own_other = own_other + high(from_right_other) + high(from_left_other)
    over = sent(low(own_other), ACROSS)
    first, second = call(
        final_kernel, [shape((depth, width)), shape((width // 16, bins))], [VMEM] * 4
    )(own_same, from_left_same, from_right_same, over)
    return (targets.reshape(-1), first[None], second[None])


def solution(mesh):
    placed = (
        P("rep", None),
        P("rep", None),
        P("rep", None, None),
        P(),
        P("rep"),
        P("rep"),
        P("rep"),
        P("rep"),
        P("ens", None, None),
        P("ens", None, None),
    )
    return jax.shard_map(
        update,
        mesh=mesh,
        in_specs=placed,
        out_specs=(P("rep"), P("ens", "rep", None), P("ens", "rep", None)),
        check_vma=False,
    )
```

profile of v0, /device:TPU:0, one launch (start us, length us, event | category | flops | bytes accessed | tf_op | source)
XLA Modules:
  0.0 73.9 jit_solution(1593811884940653001)
XLA Ops:
  0.6 0.0 copy-start
  0.6 0.0 copy-start.1
  0.7 0.0 copy-start.2
  0.7 0.0 copy-start.3
  0.7 0.0 copy-start.4
  0.7 0.0 copy-start.5
  0.7 4.5 %shard_map.121 = (f32[8,16,128]{2,1,0:T(8,128)}, bf16[4096,512]{1,0:T(8,128)(2,1)S(1)}) custom-call(bf16[256,4096]{1,0:T(8,128)(2,1)} %buffer_ref.1, bf16[4096,512]{1,0:T(8,128)(2,1)} %bitcast.21, bf16[512,256]{1,0:T(8,128)(2,1)} %bitcast.14, s32[16,128]{1,0:T(8,128)} %bitcast.23), custom_call_target="tpu_custom_call" | custom-call | flops 1073741824 | bytes 6291456 | tf_op jit(solution)/shard_map/pallas_call | solution.py:301
  5.2 20.4 %all_to_all.5 = f32[128,1,128]{2,1,0:T(1,128)S(1)} all-to-all(f32[128,1,128]{2,1,0:T(1,128)} %bitcast.22), channel_id=1, replica_groups=mesh['ens'=8,'rep'=16] {'ens','rep'}, dimensions={0} | all-to-all | bytes 131072 | tf_op jit(solution)/shard_map/all_to_all | solution.py:318
  25.7 0.0 copy-done
  25.7 0.0 copy-done.1
  25.7 0.0 copy-done.2
  25.7 0.0 copy-done.3
  25.7 0.0 copy-done.4
  25.7 0.0 copy-done.5
  25.7 6.7 %shard_map.122 = (f32[16,128]{1,0:T(8,128)}, bf16[2048,4096]{1,0:T(8,128)(2,1)S(1)}, bf16[512,2048]{1,0:T(8,128)(2,1)S(1)}, f32[512,256]{1,0:T(8,128)S(1)}, s32[8,128]{1,0:T(8,128)S(1)}) custom-call(s32[16,16]{1,0:T(8,128)S(1)} %copy-done.1, bf16[2048,4096]{1,0:T(8,128)(2,1)} %states_ref.1, bf16[4096,512]{1,0:T(8,128)(2,1)S(1)} %get-tuple-element.23.w_first, ...), custom_call_target="tpu_custom_call" | custom-call | flops 4294967296 | bytes 14680064 | tf_op jit(solution)/shard_map/pallas_call | solution.py:322
  32.4 1.4 %shard_map.123 = bf16[4,544,256]{2,1,0:T(8,128)(2,1)S(1)} custom-call(s32[8,128]{1,0:T(8,128)S(1)} %get-tuple-element.26.blocks_ref, bf16[512,2048]{1,0:T(8,128)(2,1)S(1)} %get-tuple-element.27.d_hidden_ref, bf16[2048,4096]{1,0:T(8,128)(2,1)S(1)} %get-tuple-element.28.states_ref, f32[512,256]{1,0:T(8,128)S(1)} %get-tuple-element.29.grad_ref), custom_call_target="tpu_custom_call" | custom-call | flops 1073741824 | bytes 1048576 | tf_op jit(solution)/shard_map/pallas_call | solution.py:353
  33.8 0.1 collective-permute-start
  33.9 0.7 %shard_map.127 = bf16[2,544,256]{2,1,0:T(8,128)(2,1)S(1)} custom-call(s32[8,128]{1,0:T(8,128)S(1)} %get-tuple-element.26.blocks_ref, bf16[512,2048]{1,0:T(8,128)(2,1)S(1)} %get-tuple-element.27.d_hidden_ref, bf16[2048,4096]{1,0:T(8,128)(2,1)S(1)} %get-tuple-element.28.states_ref, f32[512,256]{1,0:T(8,128)S(1)} %get-tuple-element.29.grad_ref), custom_call_target="tpu_custom_call" | custom-call | flops 536870912 | bytes 524288 | tf_op jit(solution)/shard_map/pallas_call | solution.py:353
  34.6 0.6 collective-permute-start.3
  35.2 0.9 %shard_map.125 = bf16[2,544,256]{2,1,0:T(8,128)(2,1)S(1)} custom-call(s32[8,128]{1,0:T(8,128)S(1)} %get-tuple-element.26.blocks_ref, bf16[512,2048]{1,0:T(8,128)(2,1)S(1)} %get-tuple-element.27.d_hidden_ref, bf16[2048,4096]{1,0:T(8,128)(2,1)S(1)} %get-tuple-element.28.states_ref, f32[512,256]{1,0:T(8,128)S(1)} %get-tuple-element.29.grad_ref), custom_call_target="tpu_custom_call" | custom-call | flops 536870912 | bytes 524288 | tf_op jit(solution)/shard_map/pallas_call | solution.py:353
  36.1 0.1 collective-permute-start.1
  36.3 1.1 %collective-permute-done.3.rest_0_ = bf16[2,544,256]{2,1,0:T(8,128)(2,1)S(1)} collective-permute-done((bf16[2,544,256]{2,1,0:T(8,128)(2,1)S(1)}, bf16[2,544,256]{2,1,0:T(8,128)(2,1)S(1)}, u32[]{:S(2)}, u32[]{:S(2)}) %collective-permute-start.3) | collective-permute-done | bytes 557088 | tf_op jit(solution)/shard_map/ppermute | solution.py:39
  37.4 0.8 %shard_map.128 = (bf16[544,256]{1,0:T(8,128)(2,1)S(1)}, bf16[544,256]{1,0:T(8,128)(2,1)S(1)}) custom-call(s32[8,128]{1,0:T(8,128)S(1)} %get-tuple-element.26.blocks_ref, bf16[512,2048]{1,0:T(8,128)(2,1)S(1)} %get-tuple-element.27.d_hidden_ref, bf16[2048,4096]{1,0:T(8,128)(2,1)S(1)} %get-tuple-element.28.states_ref, ...), custom_call_target="tpu_custom_call" | custom-call | flops 536870912 | bytes 524288 | tf_op jit(solution)/shard_map/pallas_call | solution.py:353
  38.2 3.0 %collective-permute-start.7 = (bf16[544,256]{1,0:T(8,128)(2,1)S(1)}, bf16[544,256]{1,0:T(8,128)(2,1)S(1)}, u32[]{:S(2)}, u32[]{:S(2)}) collective-permute-start(bf16[544,256]{1,0:T(8,128)(2,1)S(1)} %get-tuple-element.40), channel_id=1, source_target_pairs={{0,2},{1,3},{2,4},{3,5},{4,6},{5,7},{6,0},{7,1},{8,10},{9,11},{10,... | collective-permute-start | bytes 835592 | tf_op jit(solution)/shard_map/ppermute | solution.py:39
  41.2 3.2 %collective-permute-start.4 = (bf16[544,256]{1,0:T(8,128)(2,1)S(1)}, bf16[544,256]{1,0:T(8,128)(2,1)S(1)}, u32[]{:S(2)}, u32[]{:S(2)}) collective-permute-start(bf16[544,256]{1,0:T(8,128)(2,1)S(1)} %get-tuple-element.36), channel_id=1, source_target_pairs={{0,6},{1,7},{2,0},{3,1},{4,2},{5,3},{6,4},{7,5},{8,14},{9,15},{10,... | collective-permute-start | bytes 835592 | tf_op jit(solution)/shard_map/ppermute | solution.py:39
  44.4 0.0 collective-permute-done.1.rest_0_
  44.4 0.8 %shard_map.126 = (f32[544,256]{1,0:T(8,128)S(1)}, f32[544,256]{1,0:T(8,128)S(1)}) custom-call(s32[8,128]{1,0:T(8,128)S(1)} %get-tuple-element.26.blocks_ref, bf16[512,2048]{1,0:T(8,128)(2,1)S(1)} %get-tuple-element.27.d_hidden_ref, bf16[2048,4096]{1,0:T(8,128)(2,1)S(1)} %get-tuple-element.28.states_ref, f32[512,256]{1,0:T(8,128)S(1)} %get-tuple-element.29.grad_ref, ...), custom_call_target="tpu_custom_call" | custom-call | flops 536870912 | bytes 524288 | tf_op jit(solution)/shard_map/pallas_call | solution.py:353
  45.2 0.0 collective-permute-done.rest_0_
  45.3 1.8 %shard_map.124 = (f32[544,256]{1,0:T(8,128)S(1)}, bf16[544,256]{1,0:T(8,128)(2,1)S(1)}, bf16[544,256]{1,0:T(8,128)(2,1)S(1)}, f32[544,256]{1,0:T(8,128)S(1)}) custom-call(s32[8,128]{1,0:T(8,128)S(1)} %get-tuple-element.26.blocks_ref, bf16[512,2048]{1,0:T(8,128)(2,1)S(1)} %get-tuple-element.27.d_hidden_ref, ...), custom_call_target="tpu_custom_call" | custom-call | flops 1073741824 | bytes 1048576 | tf_op jit(solution)/shard_map/pallas_call | solution.py:353
  47.0 4.1 %collective-permute-done.7 = bf16[544,256]{1,0:T(8,128)(2,1)S(1)} collective-permute-done((bf16[544,256]{1,0:T(8,128)(2,1)S(1)}, bf16[544,256]{1,0:T(8,128)(2,1)S(1)}, u32[]{:S(2)}, u32[]{:S(2)}) %collective-permute-start.7) | collective-permute-done | bytes 278560 | tf_op jit(solution)/shard_map/ppermute | solution.py:39
  51.2 0.1 add_convert_fusion.1
  51.2 0.1 collective-permute-start.8
  51.3 3.2 %collective-permute-start.6 = (bf16[544,256]{1,0:T(8,128)(2,1)S(1)}, bf16[544,256]{1,0:T(8,128)(2,1)S(1)}, u32[]{:S(2)}, u32[]{:S(2)}) collective-permute-start(bf16[544,256]{1,0:T(8,128)(2,1)S(1)} %get-tuple-element.38), channel_id=1, source_target_pairs={{0,6},{1,7},{2,0},{3,1},{4,2},{5,3},{6,4},{7,5},{8,14},{9,15},{10,... | collective-permute-start | bytes 835592 | tf_op jit(solution)/shard_map/ppermute | solution.py:39
  54.5 0.0 collective-permute-start.2
  54.5 0.0 collective-permute-done.4
  54.5 0.1 add_convert_fusion.2
  54.6 3.3 %collective-permute-start.5 = (bf16[544,256]{1,0:T(8,128)(2,1)S(1)}, bf16[544,256]{1,0:T(8,128)(2,1)S(1)}, u32[]{:S(2)}, u32[]{:S(2)}) collective-permute-start(bf16[544,256]{1,0:T(8,128)(2,1)S(1)} %add_convert_fusion.2), channel_id=1, source_target_pairs={{0,6},{1,7},{2,0},{3,1},{4,2},{5,3},{6,4},{7,5},{8,14},{9,15},{10,... | collective-permute-start | bytes 835592 | tf_op jit(solution)/shard_map/ppermute | solution.py:39
  57.9 4.1 %collective-permute-done.8 = bf16[544,256]{1,0:T(8,128)(2,1)S(1)} collective-permute-done((bf16[544,256]{1,0:T(8,128)(2,1)S(1)}, bf16[544,256]{1,0:T(8,128)(2,1)S(1)}, u32[]{:S(2)}, u32[]{:S(2)}) %collective-permute-start.8) | collective-permute-done | bytes 278560 | tf_op jit(solution)/shard_map/ppermute | solution.py:39
  62.0 0.0 collective-permute-done.6
  62.0 0.1 add_convert_fusion
  62.1 6.0 %collective-permute-start.9 = (bf16[544,256]{1,0:T(8,128)(2,1)S(1)}, bf16[544,256]{1,0:T(8,128)(2,1)S(1)}, u32[]{:S(2)}, u32[]{:S(2)}) collective-permute-start(bf16[544,256]{1,0:T(8,128)(2,1)S(1)} %add_convert_fusion), channel_id=1, source_target_pairs={{0,8},{1,9},{2,10},{3,11},{4,12},{5,13},{6,14},{7,15},{8,0},{9,1},... | collective-permute-start | bytes 835592 | tf_op jit(solution)/shard_map/ppermute | solution.py:39
  68.2 0.0 collective-permute-done.2.left_ref
  68.2 0.0 collective-permute-done.5.right_ref
  68.2 4.7 %collective-permute-done.9.over_ref = bf16[544,256]{1,0:T(8,128)(2,1)S(1)} collective-permute-done((bf16[544,256]{1,0:T(8,128)(2,1)S(1)}, bf16[544,256]{1,0:T(8,128)(2,1)S(1)}, u32[]{:S(2)}, u32[]{:S(2)}) %collective-permute-start.9) | collective-permute-done | bytes 278560 | tf_op jit(solution)/shard_map/ppermute | solution.py:39
  72.9 1.0 %shard_map.129 = (f32[256,512]{1,0:T(8,128)}, f32[32,256]{1,0:T(8,128)}) custom-call(f32[544,256]{1,0:T(8,128)S(1)} %get-tuple-element.33.own_ref, bf16[544,256]{1,0:T(8,128)(2,1)S(1)} %collective-permute-done.2.left_ref, bf16[544,256]{1,0:T(8,128)(2,1)S(1)} %collective-permute-done.5.right_ref, bf16[544,256]{1,0:T(8,128)(2,1)S(1)} %collective-permute-done.9.over_ref), custom_call_target="tpu_custom_call" | custom-call | bytes 1048576 | tf_op jit(solution)/shard_map/pallas_call | solution.py:385
Async XLA Ops:
  0.6 25.0 %copy-start = (bf16[1,512,256]{2,1,0:T(8,128)(2,1)S(1)}, bf16[1,512,256]{2,1,0:T(8,128)(2,1)}, u32[]{:S(2)}) copy-start(bf16[1,512,256]{2,1,0:T(8,128)(2,1)} %param.19) | copy-start | bytes 786436
  0.6 25.0 %copy-start.1 = (s32[16,16]{1,0:T(8,128)S(1)}, s32[16,16]{1,0:T(8,128)}, u32[]{:S(2)}) copy-start(s32[16,16]{1,0:T(8,128)} %table_ref.1) | copy-start | bytes 3076
  0.7 25.0 %copy-start.2 = (s32[2048]{0:T(1024)S(1)}, s32[2048]{0:T(1024)}, u32[]{:S(2)}) copy-start(s32[2048]{0:T(1024)} %param.14) | copy-start | bytes 24580
  0.7 25.0 %copy-start.3 = (f32[2048]{0:T(1024)S(1)}, f32[2048]{0:T(1024)}, u32[]{:S(2)}) copy-start(f32[2048]{0:T(1024)} %param.15) | copy-start | bytes 24580
  0.7 25.0 %copy-start.4 = (s32[2048]{0:T(1024)S(1)}, s32[2048]{0:T(1024)}, u32[]{:S(2)}) copy-start(s32[2048]{0:T(1024)} %param.16) | copy-start | bytes 24580
  0.7 25.0 %copy-start.5 = (f32[2048]{0:T(1024)S(1)}, f32[2048]{0:T(1024)}, u32[]{:S(2)}) copy-start(f32[2048]{0:T(1024)} %param.17) | copy-start | bytes 24580
  33.8 11.5 %collective-permute-start = (bf16[4,544,256]{2,1,0:T(8,128)(2,1)S(1)}, bf16[4,544,256]{2,1,0:T(8,128)(2,1)S(1)}, u32[]{:S(2)}, u32[]{:S(2)}) collective-permute-start(bf16[4,544,256]{2,1,0:T(8,128)(2,1)S(1)} %shard_map.123), channel_id=1, source_target_pairs={{0,1},{1,0},{2,3},{3,2},{4,5},{5,4},{6,7},{7,6},{8,9},{9,8},{10,11... | collective-permute-start | bytes 3342344 | tf_op jit(solution)/shard_map/ppermute | solution.py:39
  34.6 2.8 %collective-permute-start.3 = (bf16[2,544,256]{2,1,0:T(8,128)(2,1)S(1)}, bf16[2,544,256]{2,1,0:T(8,128)(2,1)S(1)}, u32[]{:S(2)}, u32[]{:S(2)}) collective-permute-start(bf16[2,544,256]{2,1,0:T(8,128)(2,1)S(1)} %shard_map.127), channel_id=1, source_target_pairs={{0,1},{1,0},{2,3},{3,2},{4,5},{5,4},{6,7},{7,6},{8,9},{9,8},{10,11... | collective-permute-start | bytes 1671176 | tf_op jit(solution)/shard_map/ppermute | solution.py:39
  36.1 8.3 %collective-permute-start.1 = (bf16[2,544,256]{2,1,0:T(8,128)(2,1)S(1)}, bf16[2,544,256]{2,1,0:T(8,128)(2,1)S(1)}, u32[]{:S(2)}, u32[]{:S(2)}) collective-permute-start(bf16[2,544,256]{2,1,0:T(8,128)(2,1)S(1)} %shard_map.125), channel_id=1, source_target_pairs={{0,1},{1,0},{2,3},{3,2},{4,5},{5,4},{6,7},{7,6},{8,9},{9,8},{10,11... | collective-permute-start | bytes 1671176 | tf_op jit(solution)/shard_map/ppermute | solution.py:39
  38.2 12.9 %collective-permute-start.7 = (bf16[544,256]{1,0:T(8,128)(2,1)S(1)}, bf16[544,256]{1,0:T(8,128)(2,1)S(1)}, u32[]{:S(2)}, u32[]{:S(2)}) collective-permute-start(bf16[544,256]{1,0:T(8,128)(2,1)S(1)} %get-tuple-element.40), channel_id=1, source_target_pairs={{0,2},{1,3},{2,4},{3,5},{4,6},{5,7},{6,0},{7,1},{8,10},{9,11},{10,... | collective-permute-start | bytes 835592 | tf_op jit(solution)/shard_map/ppermute | solution.py:39
  41.2 13.3 %collective-permute-start.4 = (bf16[544,256]{1,0:T(8,128)(2,1)S(1)}, bf16[544,256]{1,0:T(8,128)(2,1)S(1)}, u32[]{:S(2)}, u32[]{:S(2)}) collective-permute-start(bf16[544,256]{1,0:T(8,128)(2,1)S(1)} %get-tuple-element.36), channel_id=1, source_target_pairs={{0,6},{1,7},{2,0},{3,1},{4,2},{5,3},{6,4},{7,5},{8,14},{9,15},{10,... | collective-permute-start | bytes 835592 | tf_op jit(solution)/shard_map/ppermute | solution.py:39
  51.2 10.8 %collective-permute-start.8 = (bf16[544,256]{1,0:T(8,128)(2,1)S(1)}, bf16[544,256]{1,0:T(8,128)(2,1)S(1)}, u32[]{:S(2)}, u32[]{:S(2)}) collective-permute-start(bf16[544,256]{1,0:T(8,128)(2,1)S(1)} %add_convert_fusion.1), channel_id=1, source_target_pairs={{0,2},{1,3},{2,4},{3,5},{4,6},{5,7},{6,0},{7,1},{8,10},{9,11},{10,... | collective-permute-start | bytes 835592 | tf_op jit(solution)/shard_map/ppermute | solution.py:39
  51.3 10.7 %collective-permute-start.6 = (bf16[544,256]{1,0:T(8,128)(2,1)S(1)}, bf16[544,256]{1,0:T(8,128)(2,1)S(1)}, u32[]{:S(2)}, u32[]{:S(2)}) collective-permute-start(bf16[544,256]{1,0:T(8,128)(2,1)S(1)} %get-tuple-element.38), channel_id=1, source_target_pairs={{0,6},{1,7},{2,0},{3,1},{4,2},{5,3},{6,4},{7,5},{8,14},{9,15},{10,... | collective-permute-start | bytes 835592 | tf_op jit(solution)/shard_map/ppermute | solution.py:39
  54.5 13.6 %collective-permute-start.2 = (bf16[544,256]{1,0:T(8,128)(2,1)S(1)}, bf16[544,256]{1,0:T(8,128)(2,1)S(1)}, u32[]{:S(2)}, u32[]{:S(2)}) collective-permute-start(bf16[544,256]{1,0:T(8,128)(2,1)S(1)} %get-tuple-element.34), channel_id=1, source_target_pairs={{0,2},{1,3},{2,4},{3,5},{4,6},{5,7},{6,0},{7,1},{8,10},{9,11},{10,... | collective-permute-start | bytes 835592 | tf_op jit(solution)/shard_map/ppermute | solution.py:39
  54.6 13.6 %collective-permute-start.5 = (bf16[544,256]{1,0:T(8,128)(2,1)S(1)}, bf16[544,256]{1,0:T(8,128)(2,1)S(1)}, u32[]{:S(2)}, u32[]{:S(2)}) collective-permute-start(bf16[544,256]{1,0:T(8,128)(2,1)S(1)} %add_convert_fusion.2), channel_id=1, source_target_pairs={{0,6},{1,7},{2,0},{3,1},{4,2},{5,3},{6,4},{7,5},{8,14},{9,15},{10,... | collective-permute-start | bytes 835592 | tf_op jit(solution)/shard_map/ppermute | solution.py:39
  62.1 10.7 %collective-permute-start.9 = (bf16[544,256]{1,0:T(8,128)(2,1)S(1)}, bf16[544,256]{1,0:T(8,128)(2,1)S(1)}, u32[]{:S(2)}, u32[]{:S(2)}) collective-permute-start(bf16[544,256]{1,0:T(8,128)(2,1)S(1)} %add_convert_fusion), channel_id=1, source_target_pairs={{0,8},{1,9},{2,10},{3,11},{4,12},{5,13},{6,14},{7,15},{8,0},{9,1},... | collective-permute-start | bytes 835592 | tf_op jit(solution)/shard_map/ppermute | solution.py:39
where the time goes:
time: 75 us; the launch traced here: 73.9 us
  blocking collectives  20.4 us (27%)
  starting transfers between devices  19.7 us (26%)
  Pallas kernels  18.7 us (25%)
  waiting for transfers between devices  14.1 us (19%)
  between operations  0.8 us (1%)
    all_to_all x1, blocking collectives, update(): lax.all_to_all(picked.reshape(members * owners, 1, cap), ('ens', 'rep'),...  20.4 us
    ppermute x10, starting transfers between devices, sent(): return lax.ppermute(value, 'rep', pairs)  19.7 us
    ppermute x10, waiting for transfers between devices, sent(): return lax.ppermute(value, 'rep', pairs)  14.1 us
    pallas_call x1, Pallas kernels, update(): call(member_kernel, [shape((owners, cap)), pltpu.VMEM((slots, model), BF1...  6.65 us
    pallas_call x6, Pallas kernels, pieces(): call(functools.partial(piece_kernel, steps, len(extra), stacked), out, [V...  6.46 us
    pallas_call x1, Pallas kernels, update(): call(next_kernel, [pltpu.HBM((members, owners, cap), F32), pltpu.VMEM(w_f...  4.52 us
  transfers between devices with their start and end apart: 10, of which 4 were waited for; matrix products, arithmetic and copies ran while one was open for 0% of the time, Pallas kernels for 7%

commit v1 on v0

--- a/solution.py
+++ b/solution.py
@@ -32,6 +32,7 @@
 CORE = moves(lambda y, x, c: (y, x, 1 - c))
 RIGHT = moves(lambda y, x, c: (y, (x + 1) % 4, c))
 LEFT = moves(lambda y, x, c: (y, (x + 3) % 4, c))
+FAR = moves(lambda y, x, c: (y, (x + 2) % 4, c))
 ACROSS = moves(lambda y, x, c: (1 - y, x, c))
 
 
@@ -132,7 +133,7 @@
 
 def next_kernel(
     buffer_ref, w_in_ref, w_out_ref, fetch_ref, picked_ref, w_ref, rows_ref, w_second, fetch, total,
-    found_rows, sems, small_sems,
+    sems, small_sems,
 ):
     steps = sems.shape[1]
     depth = w_in_ref.shape[0] // steps
@@ -170,11 +171,8 @@
             for half in halves
         ]
         picked = jnp.where(rows < 128, found[0], found[1])
-        for d in range(found_rows.shape[0]):
-            found_rows[d, pl.ds(i, 8), :] = picked
-    out = pltpu.make_async_copy(found_rows, picked_ref, small_sems.at[2])
-    out.start()
-    out.wait()
+        for d in range(picked_ref.shape[0]):
+            picked_ref[d, pl.ds(i, 8), :] = picked
 
 
 def member_kernel(
@@ -186,6 +184,16 @@
     me = lax.axis_index("rep")
     owners, cap = rewards_ref.shape
     blocks = gathered(counts_ref, states_ref, packed_ref, lambda b: sems.at[b])
+
+    def arrived(b):
+        gathered_block(states_ref, packed_ref, sems.at[b]).wait()
+
+    def begin(b):
+        part = pl.ds(pl.multiple_of(b * BLOCK, BLOCK), BLOCK)
+        preacts[b & 1] = jnp.dot(packed_ref[part, :], w_first[...], preferred_element_type=F32)
+
+    arrived(0)
+    begin(jnp.int32(0))
     blocks_ref[...] = jnp.full(blocks_ref.shape, blocks, jnp.int32)
     counts = table_ref[...]
     counted = jnp.sum(counts).astype(F32)
@@ -203,13 +211,6 @@
     bins = lax.broadcasted_iota(jnp.int32, (grad_ref.shape[1], BLOCK), 0).astype(F32)
     w_out = w_second[...]
     w_out_turned = w_out.T
-
-    def arrived(b):
-        gathered_block(states_ref, packed_ref, sems.at[b]).wait()
-
-    def begin(b):
-        part = pl.ds(pl.multiple_of(b * BLOCK, BLOCK), BLOCK)
-        preacts[b & 1] = jnp.dot(packed_ref[part, :], w_first[...], preferred_element_type=F32)
 
     def finish(b):
         at = pl.ds(pl.multiple_of(b * BLOCK, BLOCK), BLOCK)
@@ -231,9 +232,6 @@
         back = jnp.dot(w_out, d_logits, preferred_element_type=F32)
         d_hidden_ref[:, at] = low(back * sigmoid_pre * (1.0 + preact * (1.0 - sigmoid_pre)))
 
-    arrived(0)
-    begin(jnp.int32(0))
-
     def step(b, carry):
         arrived(b)
         finish(b - 1)
@@ -244,13 +242,13 @@
     finish(blocks - 1)
 
 
-def piece_kernel(steps, with_recv, stacked, blocks_ref, d_hidden_ref, states_ref, grad_ref, *rest):
+def piece_kernel(steps, parts, with_recv, blocks_ref, d_hidden_ref, states_ref, grad_ref, *rest):
     recv_ref = rest[0] if with_recv else None
     out_refs, total = rest[with_recv:-1], rest[-1]
     me = lax.axis_index("rep")
     y, x, core = me >> 3, (me >> 1) & 3, me & 1
     blocks = blocks_ref[0, 0]
-    _, width, depth = total.shape
+    width, depth = d_hidden_ref.shape[0], total.shape[2]
     rows = grad_ref.shape[0] // 16
     ats = [place(y ^ dy, (x + dx) & 3, core ^ dc) for dy, dx, dc in steps]
 
@@ -263,7 +261,7 @@
                 for k in range(len(ats) - 1):
                     at = jnp.where(j == k, ats[k], at)
                 columns = pl.ds(pl.multiple_of(at * depth, depth), depth)
-                total[j] = jnp.dot(
+                total[j, pl.ds(0, width), :] = jnp.dot(
                     d_hidden_ref[:, :deep], states_ref[:deep, columns], preferred_element_type=F32
                 )
                 return carry
@@ -271,19 +269,18 @@
             lax.fori_loop(0, len(ats), piece, 0)
 
     for j, at in enumerate(ats):
-        first = total[j]
-        second = grad_ref[pl.ds(pl.multiple_of(at * rows, rows), rows), :]
-        if with_recv:
-            first = first + high(recv_ref[j, pl.ds(0, width), :])
-            second = second + high(recv_ref[j, pl.ds(width, rows), :])
-        out = out_refs[0].at[j] if stacked else out_refs[j]
-        out[pl.ds(0, width), :] = first.astype(out.dtype)
-        out[pl.ds(width, rows), :] = second.astype(out.dtype)
-
-
-def final_kernel(own_ref, left_ref, right_ref, over_ref, first_ref, second_ref):
+        total[j, pl.ds(width, rows), :] = grad_ref[pl.ds(pl.multiple_of(at * rows, rows), rows), :]
+    if parts is None:
+        out_refs[0][...] = low(total[...])
+        return
+    for out, (j, first, last, _) in zip(out_refs, parts):
+        part = pl.ds(first, last - first)
+        out[...] = (total[j, part, :] + high(recv_ref[j, part, :])).astype(out.dtype)
+
+
+def final_kernel(own_ref, far_ref, first_ref, second_ref):
     width = first_ref.shape[1]
-    total = own_ref[...] + high(left_ref[...]) + high(right_ref[...]) + high(over_ref[...])
+    total = own_ref[...] + high(far_ref[...])
     first_ref[...] = total[:width].T
     second_ref[...] = total[width:]
 
@@ -300,18 +297,16 @@
 
     picked, w_kept = call(
         next_kernel,
-        [pltpu.HBM((members, owners, cap), F32), pltpu.VMEM(w_first.shape, BF16)],
+        [pltpu.VMEM((members, owners, cap), F32), pltpu.VMEM(w_first.shape, BF16)],
         [HBM] * 4,
         [
             pltpu.VMEM(buffer.shape, BF16),
             pltpu.VMEM(w_second.shape, BF16),
             pltpu.VMEM((owners, cap), jnp.int32),
             pltpu.VMEM((buffer.shape[0], width), F32),
-            pltpu.VMEM((members, owners, cap), F32),
             pltpu.SemaphoreType.DMA((2, 8)),
-            pltpu.SemaphoreType.DMA((3,)),
+            pltpu.SemaphoreType.DMA((2,)),
         ],
-        out_specs=[HBM, VMEM],
         flops=2 * buffer.shape[0] * model * width,
         bytes_moved=6 << 20,
     )(*[in_hbm(a) for a in (buffer, w_first, w_second, fetch_rows[0])])
@@ -342,49 +337,51 @@
     depth = model // 16
     tall = width + width // 16
 
-    def pieces(source, steps, dtypes=None, recv=None):
-        stacked = dtypes is None
+    def pieces(steps, parts=None, recv=None):
         out = (
             shape((len(steps), tall, depth), BF16)
-            if stacked
-            else [shape((tall, depth), t) for t in dtypes]
+            if parts is None
+            else [shape((last - first, depth), dtype) for _, first, last, dtype in parts]
         )
         extra = () if recv is None else (recv,)
+        core = 0 if extra else 1
         return call(
-            functools.partial(piece_kernel, steps, len(extra), stacked),
+            functools.partial(piece_kernel, [(*s, core) for s in steps], parts, len(extra)),
             out,
             [VMEM] * (4 + len(extra)),
-            [pltpu.VMEM((len(steps), width, depth), F32)],
+            [pltpu.VMEM((len(steps), tall, depth), F32)],
             flops=len(steps) * slots * width * depth,
             bytes_moved=len(steps) << 18,
-        )(blocks, source, packed, grad_second, *extra)
-
-    far = [(1, 2), (0, 2)]
-    near = [(1, 1), (1, 3), (0, 1), (0, 3)]
+        )(blocks, d_hidden, packed, grad_second, *extra)
+
+    other = [(1, 2), (1, 1), (1, 3)]
+    same = [(0, 2), (0, 1), (0, 3)]
     own = [(1, 0), (0, 0)]
-    theirs = lambda group: tuple((*g, 1) for g in group)
-    ours = lambda group: tuple((*g, 0) for g in group)
-
-    away_far = sent(pieces(d_hidden, theirs(far)), CORE)
-    away_near = sent(pieces(d_hidden, theirs(near)), CORE)
-    far_other, far_same = pieces(d_hidden, ours(far), (BF16, BF16), away_far)
-    from_left_far = sent(far_other, RIGHT)
-    from_right_far = sent(far_same, LEFT)
-    away_own = sent(pieces(d_hidden, theirs(own)), CORE)
-    right_other, left_other, right_same, left_same = pieces(
-        d_hidden, ours(near), (F32, BF16, BF16, F32), away_near
-    )
+
+    away_other = sent(pieces(other), CORE)
+    away_same = sent(pieces(same), CORE)
+    far_other, right_other, left_other = pieces(
+        other, [(j, 0, tall, BF16) for j in range(3)], away_other
+    )
+    across_far = sent(far_other, ACROSS)
+    from_left_other = sent(right_other, RIGHT)
     from_right_other = sent(left_other, LEFT)
-    own_other, own_same = pieces(d_hidden, ours(own), (F32, F32), away_own)
-    right_other, left_same, own_same = after(right_other, left_same, own_same)
-    from_left_other = sent(low(right_other + high(from_left_far)), RIGHT)
-    from_right_same = sent(low(left_same + high(from_right_far)), LEFT)
+    away_own = sent(pieces(own), CORE)
+    far_same, right_same, left_same = pieces(
+        same, [(j, 0, tall, dtype) for j, dtype in enumerate((F32, BF16, BF16))], away_same
+    )
     from_left_same = sent(right_same, RIGHT)
-    own_other = own_other + high(from_right_other) + high(from_left_other)
+    from_right_same = sent(left_same, LEFT)
+    own_other, own_same = pieces(own, [(j, 0, tall, F32) for j in range(2)], away_own)
+    far_same, own_other, own_same = after(far_same, own_other, own_same)
+    from_far = sent(low(far_same + high(across_far)), FAR)
+    own_other = own_other + high(from_left_other) + high(from_right_other)
     over = sent(low(own_other), ACROSS)
+    own_same = own_same + high(from_left_same) + high(from_right_same) + high(over)
+    own_same, from_far = after(own_same, from_far)
     first, second = call(
-        final_kernel, [shape((depth, width)), shape((width // 16, bins))], [VMEM] * 4
-    )(own_same, from_left_same, from_right_same, over)
+        final_kernel, [shape((depth, width)), shape((width // 16, bins))], [VMEM] * 2
+    )(own_same, from_far)
     return (targets.reshape(-1), first[None], second[None])
 
 

time: 75 us -> 73.7 us (0.983)
  transfers between devices with their start and end apart: 10 -> 10, of which waited for: 4 -> 3; matrix products, arithmetic and copies ran while one was open for 0% -> 0% of each run, Pallas kernels for 7% -> 8%
where the time goes in v1:
time: 73.7 us; the launch traced here: 73 us
  blocking collectives  20.3 us (28%)
  starting transfers between devices  20 us (27%)
  Pallas kernels  18.2 us (25%)
  waiting for transfers between devices  13.4 us (18%)
  between operations  0.81 us (1%)
    all_to_all x1, blocking collectives, update(): lax.all_to_all(picked.reshape(members * owners, 1, cap), ('ens', 'rep'),...  20.3 us
    ppermute x10, starting transfers between devices, sent(): return lax.ppermute(value, 'rep', pairs)  20 us
    ppermute x10, waiting for transfers between devices, sent(): return lax.ppermute(value, 'rep', pairs)  13.4 us
    pallas_call x1, Pallas kernels, update(): call(member_kernel, [shape((owners, cap)), pltpu.VMEM((slots, model), BF1...  6.69 us
    pallas_call x6, Pallas kernels, pieces(): call(functools.partial(piece_kernel, [(*s, core) for s in steps], parts,...  6.61 us
    pallas_call x1, Pallas kernels, update(): call(next_kernel, [pltpu.VMEM((members, owners, cap), F32), pltpu.VMEM(w_...  3.88 us
  transfers between devices with their start and end apart: 10, of which 3 were waited for; matrix products, arithmetic and copies ran while one was open for 0% of the time, Pallas kernels for 8%

profile of v1, /device:TPU:0, one launch (start us, length us, event | category | flops | bytes accessed | tf_op | source)
XLA Modules:
  0.0 73.0 jit_solution(15767572828254336258)
XLA Ops:
  0.6 0.0 copy-start
  0.6 0.0 copy-start.5
  0.7 0.0 copy-start.4
  0.7 0.0 copy-start.3
  0.7 0.0 copy-start.2
  0.7 0.0 copy-start.1
  0.7 3.9 %shard_map.121 = (f32[8,16,128]{2,1,0:T(8,128)S(1)}, bf16[4096,512]{1,0:T(8,128)(2,1)S(1)}) custom-call(bf16[256,4096]{1,0:T(8,128)(2,1)} %buffer_ref.1, bf16[4096,512]{1,0:T(8,128)(2,1)} %bitcast.22, bf16[512,256]{1,0:T(8,128)(2,1)} %bitcast.14, s32[16,128]{1,0:T(8,128)} %bitcast.23), custom_call_target="tpu_custom_call" | custom-call | flops 1073741824 | bytes 6291456 | tf_op jit(solution)/shard_map/pallas_call | solution.py:298
  4.6 20.3 %all_to_all.5 = f32[128,1,128]{2,1,0:T(1,128)S(1)} all-to-all(f32[128,1,128]{2,1,0:T(1,128)S(1)} %bitcast.17), channel_id=1, replica_groups=mesh['ens'=8,'rep'=16] {'ens','rep'}, dimensions={0} | all-to-all | bytes 131072 | tf_op jit(solution)/shard_map/all_to_all | solution.py:313
  24.9 0.0 copy-done
  24.9 0.0 copy-done.5
  24.9 0.0 copy-done.4
  24.9 0.0 copy-done.3
  24.9 0.0 copy-done.2
  24.9 0.0 copy-done.1
  24.9 6.7 %shard_map.122 = (f32[16,128]{1,0:T(8,128)}, bf16[2048,4096]{1,0:T(8,128)(2,1)S(1)}, bf16[512,2048]{1,0:T(8,128)(2,1)S(1)}, f32[512,256]{1,0:T(8,128)S(1)}, s32[8,128]{1,0:T(8,128)S(1)}) custom-call(s32[16,16]{1,0:T(8,128)S(1)} %copy-done.1, bf16[2048,4096]{1,0:T(8,128)(2,1)} %states_ref.1, bf16[4096,512]{1,0:T(8,128)(2,1)S(1)} %get-tuple-element.25.w_first, ...), custom_call_target="tpu_custom_call" | custom-call | flops 4294967296 | bytes 14680064 | tf_op jit(solution)/shard_map/pallas_call | solution.py:317
  31.6 1.1 %shard_map.127 = bf16[3,544,256]{2,1,0:T(8,128)(2,1)S(1)} custom-call(s32[8,128]{1,0:T(8,128)S(1)} %get-tuple-element.28.blocks_ref, bf16[512,2048]{1,0:T(8,128)(2,1)S(1)} %get-tuple-element.29.d_hidden_ref, bf16[2048,4096]{1,0:T(8,128)(2,1)S(1)} %get-tuple-element.30.states_ref, f32[512,256]{1,0:T(8,128)S(1)} %get-tuple-element.31.grad_ref), custom_call_target="tpu_custom_call" | custom-call | flops 805306368 | bytes 786432 | tf_op jit(solution)/shard_map/pallas_call | solution.py:348
  32.7 0.1 collective-permute-start.4
  32.8 1.1 %shard_map.123 = bf16[3,544,256]{2,1,0:T(8,128)(2,1)S(1)} custom-call(s32[8,128]{1,0:T(8,128)S(1)} %get-tuple-element.28.blocks_ref, bf16[512,2048]{1,0:T(8,128)(2,1)S(1)} %get-tuple-element.29.d_hidden_ref, bf16[2048,4096]{1,0:T(8,128)(2,1)S(1)} %get-tuple-element.30.states_ref, f32[512,256]{1,0:T(8,128)S(1)} %get-tuple-element.31.grad_ref), custom_call_target="tpu_custom_call" | custom-call | flops 805306368 | bytes 786432 | tf_op jit(solution)/shard_map/pallas_call | solution.py:348
  33.9 0.6 collective-permute-start
  34.5 0.9 %shard_map.125 = bf16[2,544,256]{2,1,0:T(8,128)(2,1)S(1)} custom-call(s32[8,128]{1,0:T(8,128)S(1)} %get-tuple-element.28.blocks_ref, bf16[512,2048]{1,0:T(8,128)(2,1)S(1)} %get-tuple-element.29.d_hidden_ref, bf16[2048,4096]{1,0:T(8,128)(2,1)S(1)} %get-tuple-element.30.states_ref, f32[512,256]{1,0:T(8,128)S(1)} %get-tuple-element.31.grad_ref), custom_call_target="tpu_custom_call" | custom-call | flops 536870912 | bytes 524288 | tf_op jit(solution)/shard_map/pallas_call | solution.py:348
  35.4 0.1 collective-permute-start.1
  35.5 0.0 collective-permute-done.4.rest_0_
  35.5 1.3 %shard_map.128 = (bf16[544,256]{1,0:T(8,128)(2,1)S(1)}, bf16[544,256]{1,0:T(8,128)(2,1)S(1)}, bf16[544,256]{1,0:T(8,128)(2,1)S(1)}) custom-call(s32[8,128]{1,0:T(8,128)S(1)} %get-tuple-element.28.blocks_ref, bf16[512,2048]{1,0:T(8,128)(2,1)S(1)} %get-tuple-element.29.d_hidden_ref, bf16[2048,4096]{1,0:T(8,128)(2,1)S(1)} %get-tuple-element.30.states_ref, ...), custom_call_target="tpu_custom_call" | custom-call | flops 805306368 | bytes 786432 | tf_op jit(solution)/shard_map/pallas_call | solution.py:348
  36.8 3.4 %collective-permute-start.5 = (bf16[544,256]{1,0:T(8,128)(2,1)S(1)}, bf16[544,256]{1,0:T(8,128)(2,1)S(1)}, u32[]{:S(2)}, u32[]{:S(2)}) collective-permute-start(bf16[544,256]{1,0:T(8,128)(2,1)S(1)} %get-tuple-element.39), channel_id=1, source_target_pairs={{0,2},{1,3},{2,4},{3,5},{4,6},{5,7},{6,0},{7,1},{8,10},{9,11},{10,... | collective-permute-start | bytes 835592 | tf_op jit(solution)/shard_map/ppermute | solution.py:40
  40.1 3.4 %collective-permute-start.6 = (bf16[544,256]{1,0:T(8,128)(2,1)S(1)}, bf16[544,256]{1,0:T(8,128)(2,1)S(1)}, u32[]{:S(2)}, u32[]{:S(2)}) collective-permute-start(bf16[544,256]{1,0:T(8,128)(2,1)S(1)} %get-tuple-element.40), channel_id=1, source_target_pairs={{0,6},{1,7},{2,0},{3,1},{4,2},{5,3},{6,4},{7,5},{8,14},{9,15},{10,... | collective-permute-start | bytes 835592 | tf_op jit(solution)/shard_map/ppermute | solution.py:40
  43.6 0.0 collective-permute-done.1.rest_0_
  43.6 0.8 %shard_map.126 = (f32[544,256]{1,0:T(8,128)S(1)}, f32[544,256]{1,0:T(8,128)S(1)}) custom-call(s32[8,128]{1,0:T(8,128)S(1)} %get-tuple-element.28.blocks_ref, bf16[512,2048]{1,0:T(8,128)(2,1)S(1)} %get-tuple-element.29.d_hidden_ref, bf16[2048,4096]{1,0:T(8,128)(2,1)S(1)} %get-tuple-element.30.states_ref, f32[512,256]{1,0:T(8,128)S(1)} %get-tuple-element.31.grad_ref, ...), custom_call_target="tpu_custom_call" | custom-call | flops 536870912 | bytes 524288 | tf_op jit(solution)/shard_map/pallas_call | solution.py:348
  44.4 0.0 collective-permute-done.rest_0_
  44.4 1.5 %shard_map.124 = (f32[544,256]{1,0:T(8,128)S(1)}, bf16[544,256]{1,0:T(8,128)(2,1)S(1)}, bf16[544,256]{1,0:T(8,128)(2,1)S(1)}) custom-call(s32[8,128]{1,0:T(8,128)S(1)} %get-tuple-element.28.blocks_ref, bf16[512,2048]{1,0:T(8,128)(2,1)S(1)} %get-tuple-element.29.d_hidden_ref, bf16[2048,4096]{1,0:T(8,128)(2,1)S(1)} %get-tuple-element.30.states_ref, ...), custom_call_target="tpu_custom_call" | custom-call | flops 805306368 | bytes 786432 | tf_op jit(solution)/shard_map/pallas_call | solution.py:348
  45.9 0.1 collective-permute-start.2
  46.0 3.2 %collective-permute-start.3 = (bf16[544,256]{1,0:T(8,128)(2,1)S(1)}, bf16[544,256]{1,0:T(8,128)(2,1)S(1)}, u32[]{:S(2)}, u32[]{:S(2)}) collective-permute-start(bf16[544,256]{1,0:T(8,128)(2,1)S(1)} %get-tuple-element.37), channel_id=1, source_target_pairs={{0,6},{1,7},{2,0},{3,1},{4,2},{5,3},{6,4},{7,5},{8,14},{9,15},{10,... | collective-permute-start | bytes 835592 | tf_op jit(solution)/shard_map/ppermute | solution.py:40
  49.2 7.0 %collective-permute-start.8 = (bf16[544,256]{1,0:T(8,128)(2,1)S(1)}, bf16[544,256]{1,0:T(8,128)(2,1)S(1)}, u32[]{:S(2)}, u32[]{:S(2)}) collective-permute-start(bf16[544,256]{1,0:T(8,128)(2,1)S(1)} %get-tuple-element.42), channel_id=1, source_target_pairs={{0,8},{1,9},{2,10},{3,11},{4,12},{5,13},{6,14},{7,15},{8,0},{9,1},... | collective-permute-start | bytes 835592 | tf_op jit(solution)/shard_map/ppermute | solution.py:40
  56.2 0.0 collective-permute-done.5
  56.2 0.0 collective-permute-done.6
  56.2 0.1 add_convert_fusion.1
  56.3 1.1 %collective-permute-start.7 = (bf16[544,256]{1,0:T(8,128)(2,1)S(1)}, bf16[544,256]{1,0:T(8,128)(2,1)S(1)}, u32[]{:S(2)}, u32[]{:S(2)}) collective-permute-start(bf16[544,256]{1,0:T(8,128)(2,1)S(1)} %add_convert_fusion.1), channel_id=1, source_target_pairs={{0,8},{1,9},{2,10},{3,11},{4,12},{5,13},{6,14},{7,15},{8,0},{9,1},... | collective-permute-start | bytes 835592 | tf_op jit(solution)/shard_map/ppermute | solution.py:40
  57.5 6.3 %collective-permute-done.8 = bf16[544,256]{1,0:T(8,128)(2,1)S(1)} collective-permute-done((bf16[544,256]{1,0:T(8,128)(2,1)S(1)}, bf16[544,256]{1,0:T(8,128)(2,1)S(1)}, u32[]{:S(2)}, u32[]{:S(2)}) %collective-permute-start.8) | collective-permute-done | bytes 278560 | tf_op jit(solution)/shard_map/ppermute | solution.py:40
  63.7 0.1 add_convert_fusion
  63.8 0.9 %collective-permute-start.9 = (bf16[544,256]{1,0:T(8,128)(2,1)S(1)}, bf16[544,256]{1,0:T(8,128)(2,1)S(1)}, u32[]{:S(2)}, u32[]{:S(2)}) collective-permute-start(bf16[544,256]{1,0:T(8,128)(2,1)S(1)} %add_convert_fusion), channel_id=1, source_target_pairs={{0,4},{1,5},{2,6},{3,7},{4,0},{5,1},{6,2},{7,3},{8,12},{9,13},{10,... | collective-permute-start | bytes 835592 | tf_op jit(solution)/shard_map/ppermute | solution.py:40
  64.8 0.0 collective-permute-done.2
  64.8 0.0 collective-permute-done.3
  64.8 3.9 %collective-permute-done.7 = bf16[544,256]{1,0:T(8,128)(2,1)S(1)} collective-permute-done((bf16[544,256]{1,0:T(8,128)(2,1)S(1)}, bf16[544,256]{1,0:T(8,128)(2,1)S(1)}, u32[]{:S(2)}, u32[]{:S(2)}) %collective-permute-start.7) | collective-permute-done | bytes 278560 | tf_op jit(solution)/shard_map/ppermute | solution.py:40
  68.7 0.1 convert_add_fusion.own_ref
  68.8 3.2 %collective-permute-done.9.far_ref = bf16[544,256]{1,0:T(8,128)(2,1)S(1)} collective-permute-done((bf16[544,256]{1,0:T(8,128)(2,1)S(1)}, bf16[544,256]{1,0:T(8,128)(2,1)S(1)}, u32[]{:S(2)}, u32[]{:S(2)}) %collective-permute-start.9) | collective-permute-done | bytes 278560 | tf_op jit(solution)/shard_map/ppermute | solution.py:40
  72.0 1.0 %shard_map.129 = (f32[256,512]{1,0:T(8,128)}, f32[32,256]{1,0:T(8,128)}) custom-call(f32[544,256]{1,0:T(8,128)S(1)} %convert_add_fusion.own_ref, bf16[544,256]{1,0:T(8,128)(2,1)S(1)} %collective-permute-done.9.far_ref), custom_call_target="tpu_custom_call" | custom-call | bytes 1048576 | tf_op jit(solution)/shard_map/pallas_call | solution.py:382
Async XLA Ops:
  0.6 24.3 %copy-start = (bf16[1,512,256]{2,1,0:T(8,128)(2,1)S(1)}, bf16[1,512,256]{2,1,0:T(8,128)(2,1)}, u32[]{:S(2)}) copy-start(bf16[1,512,256]{2,1,0:T(8,128)(2,1)} %param.19) | copy-start | bytes 786436
  0.6 24.2 %copy-start.5 = (f32[2048]{0:T(1024)S(1)}, f32[2048]{0:T(1024)}, u32[]{:S(2)}) copy-start(f32[2048]{0:T(1024)} %param.17) | copy-start | bytes 24580
  0.7 24.2 %copy-start.4 = (s32[2048]{0:T(1024)S(1)}, s32[2048]{0:T(1024)}, u32[]{:S(2)}) copy-start(s32[2048]{0:T(1024)} %param.16) | copy-start | bytes 24580
  0.7 24.2 %copy-start.3 = (f32[2048]{0:T(1024)S(1)}, f32[2048]{0:T(1024)}, u32[]{:S(2)}) copy-start(f32[2048]{0:T(1024)} %param.15) | copy-start | bytes 24580
  0.7 24.2 %copy-start.2 = (s32[2048]{0:T(1024)S(1)}, s32[2048]{0:T(1024)}, u32[]{:S(2)}) copy-start(s32[2048]{0:T(1024)} %param.14) | copy-start | bytes 24580
  0.7 24.2 %copy-start.1 = (s32[16,16]{1,0:T(8,128)S(1)}, s32[16,16]{1,0:T(8,128)}, u32[]{:S(2)}) copy-start(s32[16,16]{1,0:T(8,128)} %table_ref.1) | copy-start | bytes 3076
  32.7 2.8 %collective-permute-start.4 = (bf16[3,544,256]{2,1,0:T(8,128)(2,1)S(1)}, bf16[3,544,256]{2,1,0:T(8,128)(2,1)S(1)}, u32[]{:S(2)}, u32[]{:S(2)}) collective-permute-start(bf16[3,544,256]{2,1,0:T(8,128)(2,1)S(1)} %shard_map.127), channel_id=1, source_target_pairs={{0,1},{1,0},{2,3},{3,2},{4,5},{5,4},{6,7},{7,6},{8,9},{9,8},{10,11... | collective-permute-start | bytes 2506760 | tf_op jit(solution)/shard_map/ppermute | solution.py:40
  33.9 10.5 %collective-permute-start = (bf16[3,544,256]{2,1,0:T(8,128)(2,1)S(1)}, bf16[3,544,256]{2,1,0:T(8,128)(2,1)S(1)}, u32[]{:S(2)}, u32[]{:S(2)}) collective-permute-start(bf16[3,544,256]{2,1,0:T(8,128)(2,1)S(1)} %shard_map.123), channel_id=1, source_target_pairs={{0,1},{1,0},{2,3},{3,2},{4,5},{5,4},{6,7},{7,6},{8,9},{9,8},{10,11... | collective-permute-start | bytes 2506760 | tf_op jit(solution)/shard_map/ppermute | solution.py:40
  35.4 8.2 %collective-permute-start.1 = (bf16[2,544,256]{2,1,0:T(8,128)(2,1)S(1)}, bf16[2,544,256]{2,1,0:T(8,128)(2,1)S(1)}, u32[]{:S(2)}, u32[]{:S(2)}) collective-permute-start(bf16[2,544,256]{2,1,0:T(8,128)(2,1)S(1)} %shard_map.125), channel_id=1, source_target_pairs={{0,1},{1,0},{2,3},{3,2},{4,5},{5,4},{6,7},{7,6},{8,9},{9,8},{10,11... | collective-permute-start | bytes 1671176 | tf_op jit(solution)/shard_map/ppermute | solution.py:40
  36.8 19.4 %collective-permute-start.5 = (bf16[544,256]{1,0:T(8,128)(2,1)S(1)}, bf16[544,256]{1,0:T(8,128)(2,1)S(1)}, u32[]{:S(2)}, u32[]{:S(2)}) collective-permute-start(bf16[544,256]{1,0:T(8,128)(2,1)S(1)} %get-tuple-element.39), channel_id=1, source_target_pairs={{0,2},{1,3},{2,4},{3,5},{4,6},{5,7},{6,0},{7,1},{8,10},{9,11},{10,... | collective-permute-start | bytes 835592 | tf_op jit(solution)/shard_map/ppermute | solution.py:40
  40.1 16.1 %collective-permute-start.6 = (bf16[544,256]{1,0:T(8,128)(2,1)S(1)}, bf16[544,256]{1,0:T(8,128)(2,1)S(1)}, u32[]{:S(2)}, u32[]{:S(2)}) collective-permute-start(bf16[544,256]{1,0:T(8,128)(2,1)S(1)} %get-tuple-element.40), channel_id=1, source_target_pairs={{0,6},{1,7},{2,0},{3,1},{4,2},{5,3},{6,4},{7,5},{8,14},{9,15},{10,... | collective-permute-start | bytes 835592 | tf_op jit(solution)/shard_map/ppermute | solution.py:40
  45.9 18.9 %collective-permute-start.2 = (bf16[544,256]{1,0:T(8,128)(2,1)S(1)}, bf16[544,256]{1,0:T(8,128)(2,1)S(1)}, u32[]{:S(2)}, u32[]{:S(2)}) collective-permute-start(bf16[544,256]{1,0:T(8,128)(2,1)S(1)} %get-tuple-element.36), channel_id=1, source_target_pairs={{0,2},{1,3},{2,4},{3,5},{4,6},{5,7},{6,0},{7,1},{8,10},{9,11},{10,... | collective-permute-start | bytes 835592 | tf_op jit(solution)/shard_map/ppermute | solution.py:40
  46.0 18.8 %collective-permute-start.3 = (bf16[544,256]{1,0:T(8,128)(2,1)S(1)}, bf16[544,256]{1,0:T(8,128)(2,1)S(1)}, u32[]{:S(2)}, u32[]{:S(2)}) collective-permute-start(bf16[544,256]{1,0:T(8,128)(2,1)S(1)} %get-tuple-element.37), channel_id=1, source_target_pairs={{0,6},{1,7},{2,0},{3,1},{4,2},{5,3},{6,4},{7,5},{8,14},{9,15},{10,... | collective-permute-start | bytes 835592 | tf_op jit(solution)/shard_map/ppermute | solution.py:40
  49.2 14.5 %collective-permute-start.8 = (bf16[544,256]{1,0:T(8,128)(2,1)S(1)}, bf16[544,256]{1,0:T(8,128)(2,1)S(1)}, u32[]{:S(2)}, u32[]{:S(2)}) collective-permute-start(bf16[544,256]{1,0:T(8,128)(2,1)S(1)} %get-tuple-element.42), channel_id=1, source_target_pairs={{0,8},{1,9},{2,10},{3,11},{4,12},{5,13},{6,14},{7,15},{8,0},{9,1},... | collective-permute-start | bytes 835592 | tf_op jit(solution)/shard_map/ppermute | solution.py:40
  56.3 12.3 %collective-permute-start.7 = (bf16[544,256]{1,0:T(8,128)(2,1)S(1)}, bf16[544,256]{1,0:T(8,128)(2,1)S(1)}, u32[]{:S(2)}, u32[]{:S(2)}) collective-permute-start(bf16[544,256]{1,0:T(8,128)(2,1)S(1)} %add_convert_fusion.1), channel_id=1, source_target_pairs={{0,8},{1,9},{2,10},{3,11},{4,12},{5,13},{6,14},{7,15},{8,0},{9,1},... | collective-permute-start | bytes 835592 | tf_op jit(solution)/shard_map/ppermute | solution.py:40
  63.8 8.2 %collective-permute-start.9 = (bf16[544,256]{1,0:T(8,128)(2,1)S(1)}, bf16[544,256]{1,0:T(8,128)(2,1)S(1)}, u32[]{:S(2)}, u32[]{:S(2)}) collective-permute-start(bf16[544,256]{1,0:T(8,128)(2,1)S(1)} %add_convert_fusion), channel_id=1, source_target_pairs={{0,4},{1,5},{2,6},{3,7},{4,0},{5,1},{6,2},{7,3},{8,12},{9,13},{10,... | collective-permute-start | bytes 835592 | tf_op jit(solution)/shard_map/ppermute | solution.py:40

commit v2 on v1

--- a/solution.py
+++ b/solution.py
@@ -84,44 +84,57 @@
     return (count + (UNIT - 1)) >> 4
 
 
-def gathered(counts_ref, states_ref, packed_ref, sem_at):
+def run_copy(table, states_ref, packed_ref, sem, position):
+    source = pl.multiple_of(table[0, position] * UNIT, UNIT)
+    target = pl.multiple_of(position * UNIT, UNIT)
+    return pltpu.make_async_copy(
+        states_ref.at[pl.ds(source, UNIT)],
+        packed_ref.at[pl.ds(target, UNIT)],
+        sem,
+    )
+
+
+def listed(counts, table, start_first):
     me = lax.axis_index("rep")
-    owners = counts_ref.shape[0]
-    runs = states_ref.shape[0] // owners // UNIT
-
-    def start(source, position):
-        pltpu.make_async_copy(
-            states_ref.at[pl.ds(pl.multiple_of(source * UNIT, UNIT), UNIT)],
-            packed_ref.at[pl.ds(pl.multiple_of(position * UNIT, UNIT), UNIT)],
-            sem_at(position >> 4),
-        ).start()
+    owners = counts.shape[0]
+    runs = table.shape[1] // owners
+    per_block = BLOCK // UNIT
+
+    def put(source, position):
+        table[0, position] = source
+
+        @pl.when(position < per_block)
+        def _():
+            start_first(position)
 
     def owner(o, position):
+        count = counts[o, me]
+        table[1, o] = count
+
         def unit(u, position):
-            start(o * runs + u, position)
+            put(o * runs + u, position)
             return position + 1
 
-        return lax.fori_loop(0, units_of(counts_ref[o, me]), unit, position)
+        return lax.fori_loop(0, units_of(count), unit, position)
 
     units = lax.fori_loop(0, owners, owner, jnp.int32(0))
-    blocks = (units + (BLOCK // UNIT - 1)) >> 4
-    lax.fori_loop(units, blocks * (BLOCK // UNIT), lambda p, c: (start(0, p), c)[1], 0)
-    return blocks
+    blocks = (units + (per_block - 1)) >> 4
+    lax.fori_loop(units, blocks * per_block, lambda p, c: (put(0, p), c)[1], 0)
+    table[1, owners] = blocks
 
 
 def gathered_block(states_ref, packed_ref, sem):
     return pltpu.make_async_copy(states_ref.at[pl.ds(0, BLOCK)], packed_ref.at[pl.ds(0, BLOCK)], sem)
 
 
-def pack_rows(counts_ref, values, packed_refs):
-    me = lax.axis_index("rep")
+def pack_rows(table, values, packed_refs):
     owners, cap = values[0].shape
     lane = lax.broadcasted_iota(jnp.int32, (1, cap), 1)
     for ref in packed_refs:
         ref[...] = jnp.zeros_like(ref)
     start = jnp.int32(0)
     for o in range(owners):
-        count = counts_ref[o, me]
+        count = table[1, o]
         row, shift = start >> 7, start & 127
         for value, ref in zip(values, packed_refs):
             kept = jnp.where(lane < count, value[o : o + 1, :], 0.0)
@@ -132,11 +145,14 @@
 
 
 def next_kernel(
-    buffer_ref, w_in_ref, w_out_ref, fetch_ref, picked_ref, w_ref, rows_ref, w_second, fetch, total,
-    sems, small_sems,
+    buffer_ref, w_in_ref, w_out_ref, fetch_ref, counts_ref, states_ref,
+    picked_ref, w_ref, first_ref, table_ref,
+    rows_ref, w_second, fetch, total, counts, table, sems, small_sems,
 ):
     steps = sems.shape[1]
     depth = w_in_ref.shape[0] // steps
+    counted = pltpu.make_async_copy(counts_ref, counts, small_sems.at[2])
+    counted.start()
     copies = []
     for i in range(steps):
         part = pl.ds(i * depth, depth)
@@ -151,6 +167,14 @@
     wanted = pltpu.make_async_copy(fetch_ref, fetch, small_sems.at[1])
     second.start()
     wanted.start()
+    counted.wait()
+    listed(
+        counts,
+        table,
+        lambda p: run_copy(table, states_ref, first_ref, small_sems.at[3], p).start(),
+    )
+    kept_table = pltpu.make_async_copy(table, table_ref, small_sems.at[2])
+    kept_table.start()
     for i in range(steps):
         for copy in copies[i]:
             copy.wait()
@@ -173,27 +197,54 @@
         picked = jnp.where(rows < 128, found[0], found[1])
         for d in range(picked_ref.shape[0]):
             picked_ref[d, pl.ds(i, 8), :] = picked
+    kept_table.wait()
+    gathered_block(states_ref, first_ref, small_sems.at[3]).wait()
 
 
 def member_kernel(
-    counts_ref, states_ref, w_first, w_second, table_ref, best_ref,
+    listed_ref, first_ref, states_ref, w_first, w_second, table_ref, best_ref,
     actions_ref, rewards_ref, terminal_ref, returns_ref,
     targets_ref, packed_ref, d_hidden_ref, grad_ref, blocks_ref,
-    preacts, target_row, scale_row, act_row, sems,
+    raw, turned, slope, hidden_now, target_row, scale_row, act_row, table, sems, start_sems,
 ):
     me = lax.axis_index("rep")
     owners, cap = rewards_ref.shape
-    blocks = gathered(counts_ref, states_ref, packed_ref, lambda b: sems.at[b])
+    load = pltpu.make_async_copy(listed_ref, table, start_sems.at[0])
+    load.start()
+    place_first = pltpu.make_async_copy(
+        first_ref, packed_ref.at[pl.ds(0, BLOCK)], start_sems.at[1]
+    )
+    load.wait()
+    blocks = table[1, owners]
+
+    def fetch(b):
+        @pl.when(b < blocks)
+        def _():
+            for i in range(BLOCK // UNIT):
+                run_copy(
+                    table, states_ref, packed_ref, sems.at[b], b * (BLOCK // UNIT) + i
+                ).start()
+
+    fetch(jnp.int32(1))
+    fetch(jnp.int32(2))
+    place_first.start()
 
     def arrived(b):
         gathered_block(states_ref, packed_ref, sems.at[b]).wait()
 
-    def begin(b):
-        part = pl.ds(pl.multiple_of(b * BLOCK, BLOCK), BLOCK)
-        preacts[b & 1] = jnp.dot(packed_ref[part, :], w_first[...], preferred_element_type=F32)
-
-    arrived(0)
-    begin(jnp.int32(0))
+    half = w_first.shape[1] // 2
+    halves = (pl.ds(0, half), pl.ds(half, half))
+
+    def begin(b, part):
+        rows = pl.ds(pl.multiple_of(b * BLOCK, BLOCK), BLOCK)
+        raw[:, part] = jnp.dot(packed_ref[rows, :], w_first[:, part], preferred_element_type=F32)
+
+    def turn(part):
+        turned[part, :] = raw[:, part].T
+
+    for part in halves:
+        raw[:, part] = jnp.dot(first_ref[...], w_first[:, part], preferred_element_type=F32)
+        turn(part)
     blocks_ref[...] = jnp.full(blocks_ref.shape, blocks, jnp.int32)
     counts = table_ref[...]
     counted = jnp.sum(counts).astype(F32)
@@ -205,23 +256,30 @@
     targets_ref[...] = used * target
     scale = used * 2.0 * (jnp.full((owners, cap), 65536.0, F32) / counted)
     pack_rows(
-        counts_ref, [target, scale, high(actions_ref[...])], [target_row, scale_row, act_row]
+        table, [target, scale, high(actions_ref[...])], [target_row, scale_row, act_row]
     )
     grad_ref[...] = jnp.zeros_like(grad_ref)
     bins = lax.broadcasted_iota(jnp.int32, (grad_ref.shape[1], BLOCK), 0).astype(F32)
     w_out = w_second[...]
     w_out_turned = w_out.T
 
-    def finish(b):
+    def finish(b, following=None):
         at = pl.ds(pl.multiple_of(b * BLOCK, BLOCK), BLOCK)
         goal, scaled, acts = [
             jnp.concatenate([ref[pl.ds(2 * b + i, 1), :] for i in (0, 1)], axis=1)
             for ref in (target_row, scale_row, act_row)
         ]
-        preact = preacts[b & 1].T
+        preact = turned[...]
         sigmoid_pre = jax.nn.sigmoid(preact)
-        hidden = low(preact * sigmoid_pre)
+        hidden_now[...] = low(preact * sigmoid_pre)
+        slope[...] = sigmoid_pre * (1.0 + preact * (1.0 - sigmoid_pre))
+        if following is not None:
+            begin(following, halves[0])
+        hidden = hidden_now[...]
         logits = jnp.dot(w_out_turned, hidden, preferred_element_type=F32)
+        if following is not None:
+            begin(following, halves[1])
+            turn(halves[0])
         chosen = bins == acts
         taken = jax.nn.sigmoid(jnp.sum(jnp.where(chosen, logits, 0.0), axis=0, keepdims=True))
         errors = (taken - goal) * taken * (1.0 - taken) * scaled
@@ -230,16 +288,19 @@
             hidden, d_logits, (((1,), (1,)), ((), ())), preferred_element_type=F32
         )
         back = jnp.dot(w_out, d_logits, preferred_element_type=F32)
-        d_hidden_ref[:, at] = low(back * sigmoid_pre * (1.0 + preact * (1.0 - sigmoid_pre)))
+        d_hidden_ref[:, at] = low(back * slope[...])
+        if following is not None:
+            turn(halves[1])
 
     def step(b, carry):
         arrived(b)
-        finish(b - 1)
-        begin(b)
+        fetch(b + 2)
+        finish(b - 1, b)
         return carry
 
     lax.fori_loop(1, blocks, step, 0)
     finish(blocks - 1)
+    place_first.wait()
 
 
 def piece_kernel(steps, parts, with_recv, blocks_ref, d_hidden_ref, states_ref, grad_ref, *rest):
@@ -295,21 +356,33 @@
     members = lax.axis_size("ens")
     grid = lambda a: a.reshape(owners, cap)
 
-    picked, w_kept = call(
+    picked, w_kept, first_block, table = call(
         next_kernel,
-        [pltpu.VMEM((members, owners, cap), F32), pltpu.VMEM(w_first.shape, BF16)],
-        [HBM] * 4,
+        [
+            pltpu.VMEM((members, owners, cap), F32),
+            pltpu.VMEM(w_first.shape, BF16),
+            pltpu.VMEM((BLOCK, model), BF16),
+            pltpu.VMEM((8, slots // UNIT), jnp.int32),
+        ],
+        [HBM] * 6,
         [
             pltpu.VMEM(buffer.shape, BF16),
             pltpu.VMEM(w_second.shape, BF16),
             pltpu.VMEM((owners, cap), jnp.int32),
             pltpu.VMEM((buffer.shape[0], width), F32),
+            pltpu.SMEM(fetch_counts.shape, jnp.int32),
+            pltpu.SMEM((8, slots // UNIT), jnp.int32),
             pltpu.SemaphoreType.DMA((2, 8)),
-            pltpu.SemaphoreType.DMA((2,)),
+            pltpu.SemaphoreType.DMA((4,)),
         ],
         flops=2 * buffer.shape[0] * model * width,
         bytes_moved=6 << 20,
-    )(*[in_hbm(a) for a in (buffer, w_first, w_second, fetch_rows[0])])
+    )(
+        *[
+            in_hbm(a)
+            for a in (buffer, w_first, w_second, fetch_rows[0], fetch_counts, cur_states)
+        ]
+    )
     best = lax.all_to_all(
         picked.reshape(members * owners, 1, cap), ("ens", "rep"), 0, 0, tiled=True
     ).reshape(members, owners, cap)
@@ -323,14 +396,17 @@
             pltpu.VMEM((width, bins), F32),
             pltpu.VMEM((8, 128), jnp.int32),
         ],
-        [SMEM, HBM] + [VMEM] * 8,
-        [pltpu.VMEM((2, BLOCK, width), F32)]
+        [VMEM, VMEM, HBM] + [VMEM] * 8,
+        [pltpu.VMEM((BLOCK, width), F32)]
+        + [pltpu.VMEM((width, BLOCK), F32)] * 2
+        + [pltpu.VMEM((width, BLOCK), BF16)]
         + [pltpu.VMEM((owners + 8, cap), F32)] * 3
-        + [pltpu.SemaphoreType.DMA((slots // BLOCK,))],
+        + [pltpu.SMEM((8, slots // UNIT), jnp.int32)]
+        + [pltpu.SemaphoreType.DMA((slots // BLOCK,)), pltpu.SemaphoreType.DMA((2,))],
         flops=slots * model * width,
         bytes_moved=14 << 20,
     )(
-        fetch_counts, in_hbm(cur_states), w_kept, w_second, fetch_counts, best,
+        table, first_block, in_hbm(cur_states), w_kept, w_second, fetch_counts, best,
         grid(actions), grid(rewards), grid(terminal), grid(mc_return),
     )
 

time: 73.7 us -> 71.8 us (0.974)
  Pallas kernels: 18.2 us -> 16.7 us
    pallas_call x1, Pallas kernels: 6.69 us -> 5.34 us  [update(): call(member_kernel, [shape((owners, cap)), pltpu.VMEM((slots, model), BF1...]
where the time goes in v2:
time: 71.8 us; the launch traced here: 71.1 us
  blocking collectives  20.7 us (29%)
  starting transfers between devices  19.3 us (27%)
  Pallas kernels  16.7 us (23%)
  waiting for transfers between devices  13.4 us (19%)
  between operations  0.81 us (1%)
    all_to_all x1, blocking collectives, update(): lax.all_to_all(picked.reshape(members * owners, 1, cap), ('ens', 'rep'),...  20.7 us
    ppermute x10, starting transfers between devices, sent(): return lax.ppermute(value, 'rep', pairs)  19.3 us
    ppermute x10, waiting for transfers between devices, sent(): return lax.ppermute(value, 'rep', pairs)  13.4 us
    pallas_call x6, Pallas kernels, pieces(): call(functools.partial(piece_kernel, [(*s, core) for s in steps], parts,...  6.42 us
    pallas_call x1, Pallas kernels, update(): call(member_kernel, [shape((owners, cap)), pltpu.VMEM((slots, model), BF1...  5.34 us
    pallas_call x1, Pallas kernels, update(): call(next_kernel, [pltpu.VMEM((members, owners, cap), F32), pltpu.VMEM(w_...  3.92 us
  transfers between devices with their start and end apart: 10, of which 3 were waited for; matrix products, arithmetic and copies ran while one was open for 0% of the time, Pallas kernels for 8%

profile of v2, /device:TPU:0, one launch (start us, length us, event | category | flops | bytes accessed | tf_op | source)
XLA Modules:
  0.0 71.1 jit_solution(15963921939056810882)
XLA Ops:
  0.6 0.0 copy-start
  0.6 0.0 copy-start.1
  0.7 0.0 copy-start.2
  0.7 0.0 copy-start.3
  0.7 0.0 copy-start.4
  0.7 0.0 copy-start.5
  0.7 3.9 %shard_map.121 = (f32[8,16,128]{2,1,0:T(8,128)S(1)}, bf16[4096,512]{1,0:T(8,128)(2,1)S(1)}, bf16[256,4096]{1,0:T(8,128)(2,1)S(1)}, s32[8,128]{1,0:T(8,128)S(1)}) custom-call(bf16[256,4096]{1,0:T(8,128)(2,1)} %buffer_ref.1, bf16[4096,512]{1,0:T(8,128)(2,1)} %bitcast.22, bf16[512,256]{1,0:T(8,128)(2,1)} %bitcast.14, s32[16,128]{1,0:T(8,128)} %bitcast.23, ...), custom_call_target="tpu_custom_call" | custom-call | flops 1073741824 | bytes 6291456 | tf_op jit(solution)/shard_map/pallas_call | solution.py:359
  4.6 20.7 %all_to_all.5 = f32[128,1,128]{2,1,0:T(1,128)S(1)} all-to-all(f32[128,1,128]{2,1,0:T(1,128)S(1)} %bitcast.17), channel_id=1, replica_groups=mesh['ens'=8,'rep'=16] {'ens','rep'}, dimensions={0} | all-to-all | bytes 131072 | tf_op jit(solution)/shard_map/all_to_all | solution.py:386
  25.3 0.0 copy-done
  25.3 0.0 copy-done.1
  25.3 0.0 copy-done.2
  25.3 0.0 copy-done.3
  25.3 0.0 copy-done.4
  25.3 0.0 copy-done.5
  25.3 5.3 %shard_map.122 = (f32[16,128]{1,0:T(8,128)}, bf16[2048,4096]{1,0:T(8,128)(2,1)S(1)}, bf16[512,2048]{1,0:T(8,128)(2,1)S(1)}, f32[512,256]{1,0:T(8,128)S(1)}, s32[8,128]{1,0:T(8,128)S(1)}) custom-call(s32[8,128]{1,0:T(8,128)S(1)} %get-tuple-element.27.listed_ref, bf16[256,4096]{1,0:T(8,128)(2,1)S(1)} %get-tuple-element.28.first_ref, ...), custom_call_target="tpu_custom_call" | custom-call | flops 4294967296 | bytes 14680064 | tf_op jit(solution)/shard_map/pallas_call | solution.py:390
  30.7 1.1 %shard_map.127 = bf16[3,544,256]{2,1,0:T(8,128)(2,1)S(1)} custom-call(s32[8,128]{1,0:T(8,128)S(1)} %get-tuple-element.32.blocks_ref, bf16[512,2048]{1,0:T(8,128)(2,1)S(1)} %get-tuple-element.33.d_hidden_ref, bf16[2048,4096]{1,0:T(8,128)(2,1)S(1)} %get-tuple-element.34.states_ref, f32[512,256]{1,0:T(8,128)S(1)} %get-tuple-element.35.grad_ref), custom_call_target="tpu_custom_call" | custom-call | flops 805306368 | bytes 786432 | tf_op jit(solution)/shard_map/pallas_call | solution.py:424
  31.7 0.1 collective-permute-start.4
  31.8 1.1 %shard_map.123 = bf16[3,544,256]{2,1,0:T(8,128)(2,1)S(1)} custom-call(s32[8,128]{1,0:T(8,128)S(1)} %get-tuple-element.32.blocks_ref, bf16[512,2048]{1,0:T(8,128)(2,1)S(1)} %get-tuple-element.33.d_hidden_ref, bf16[2048,4096]{1,0:T(8,128)(2,1)S(1)} %get-tuple-element.34.states_ref, f32[512,256]{1,0:T(8,128)S(1)} %get-tuple-element.35.grad_ref), custom_call_target="tpu_custom_call" | custom-call | flops 805306368 | bytes 786432 | tf_op jit(solution)/shard_map/pallas_call | solution.py:424
  32.9 0.8 %collective-permute-start = (bf16[3,544,256]{2,1,0:T(8,128)(2,1)S(1)}, bf16[3,544,256]{2,1,0:T(8,128)(2,1)S(1)}, u32[]{:S(2)}, u32[]{:S(2)}) collective-permute-start(bf16[3,544,256]{2,1,0:T(8,128)(2,1)S(1)} %shard_map.123), channel_id=1, source_target_pairs={{0,1},{1,0},{2,3},{3,2},{4,5},{5,4},{6,7},{7,6},{8,9},{9,8},{10,11... | collective-permute-start | bytes 2506760 | tf_op jit(solution)/shard_map/ppermute | solution.py:40
  33.7 0.7 %shard_map.125 = bf16[2,544,256]{2,1,0:T(8,128)(2,1)S(1)} custom-call(s32[8,128]{1,0:T(8,128)S(1)} %get-tuple-element.32.blocks_ref, bf16[512,2048]{1,0:T(8,128)(2,1)S(1)} %get-tuple-element.33.d_hidden_ref, bf16[2048,4096]{1,0:T(8,128)(2,1)S(1)} %get-tuple-element.34.states_ref, f32[512,256]{1,0:T(8,128)S(1)} %get-tuple-element.35.grad_ref), custom_call_target="tpu_custom_call" | custom-call | flops 536870912 | bytes 524288 | tf_op jit(solution)/shard_map/pallas_call | solution.py:424
  34.4 0.1 collective-permute-start.1
  34.5 0.0 collective-permute-done.4.rest_0_
  34.6 1.3 %shard_map.128 = (bf16[544,256]{1,0:T(8,128)(2,1)S(1)}, bf16[544,256]{1,0:T(8,128)(2,1)S(1)}, bf16[544,256]{1,0:T(8,128)(2,1)S(1)}) custom-call(s32[8,128]{1,0:T(8,128)S(1)} %get-tuple-element.32.blocks_ref, bf16[512,2048]{1,0:T(8,128)(2,1)S(1)} %get-tuple-element.33.d_hidden_ref, bf16[2048,4096]{1,0:T(8,128)(2,1)S(1)} %get-tuple-element.34.states_ref, ...), custom_call_target="tpu_custom_call" | custom-call | flops 805306368 | bytes 786432 | tf_op jit(solution)/shard_map/pallas_call | solution.py:424
  35.8 3.1 %collective-permute-start.5 = (bf16[544,256]{1,0:T(8,128)(2,1)S(1)}, bf16[544,256]{1,0:T(8,128)(2,1)S(1)}, u32[]{:S(2)}, u32[]{:S(2)}) collective-permute-start(bf16[544,256]{1,0:T(8,128)(2,1)S(1)} %get-tuple-element.43), channel_id=1, source_target_pairs={{0,2},{1,3},{2,4},{3,5},{4,6},{5,7},{6,0},{7,1},{8,10},{9,11},{10,... | collective-permute-start | bytes 835592 | tf_op jit(solution)/shard_map/ppermute | solution.py:40
  39.0 3.2 %collective-permute-start.6 = (bf16[544,256]{1,0:T(8,128)(2,1)S(1)}, bf16[544,256]{1,0:T(8,128)(2,1)S(1)}, u32[]{:S(2)}, u32[]{:S(2)}) collective-permute-start(bf16[544,256]{1,0:T(8,128)(2,1)S(1)} %get-tuple-element.44), channel_id=1, source_target_pairs={{0,6},{1,7},{2,0},{3,1},{4,2},{5,3},{6,4},{7,5},{8,14},{9,15},{10,... | collective-permute-start | bytes 835592 | tf_op jit(solution)/shard_map/ppermute | solution.py:40
  42.1 0.0 collective-permute-done.1.rest_0_
  42.1 0.8 %shard_map.126 = (f32[544,256]{1,0:T(8,128)S(1)}, f32[544,256]{1,0:T(8,128)S(1)}) custom-call(s32[8,128]{1,0:T(8,128)S(1)} %get-tuple-element.32.blocks_ref, bf16[512,2048]{1,0:T(8,128)(2,1)S(1)} %get-tuple-element.33.d_hidden_ref, bf16[2048,4096]{1,0:T(8,128)(2,1)S(1)} %get-tuple-element.34.states_ref, f32[512,256]{1,0:T(8,128)S(1)} %get-tuple-element.35.grad_ref, ...), custom_call_target="tpu_custom_call" | custom-call | flops 536870912 | bytes 524288 | tf_op jit(solution)/shard_map/pallas_call | solution.py:424
  43.0 0.0 collective-permute-done.rest_0_
  43.0 1.5 %shard_map.124 = (f32[544,256]{1,0:T(8,128)S(1)}, bf16[544,256]{1,0:T(8,128)(2,1)S(1)}, bf16[544,256]{1,0:T(8,128)(2,1)S(1)}) custom-call(s32[8,128]{1,0:T(8,128)S(1)} %get-tuple-element.32.blocks_ref, bf16[512,2048]{1,0:T(8,128)(2,1)S(1)} %get-tuple-element.33.d_hidden_ref, bf16[2048,4096]{1,0:T(8,128)(2,1)S(1)} %get-tuple-element.34.states_ref, ...), custom_call_target="tpu_custom_call" | custom-call | flops 805306368 | bytes 786432 | tf_op jit(solution)/shard_map/pallas_call | solution.py:424
  44.4 0.1 collective-permute-start.2
  44.5 3.2 %collective-permute-start.3 = (bf16[544,256]{1,0:T(8,128)(2,1)S(1)}, bf16[544,256]{1,0:T(8,128)(2,1)S(1)}, u32[]{:S(2)}, u32[]{:S(2)}) collective-permute-start(bf16[544,256]{1,0:T(8,128)(2,1)S(1)} %get-tuple-element.41), channel_id=1, source_target_pairs={{0,6},{1,7},{2,0},{3,1},{4,2},{5,3},{6,4},{7,5},{8,14},{9,15},{10,... | collective-permute-start | bytes 835592 | tf_op jit(solution)/shard_map/ppermute | solution.py:40
  47.7 6.6 %collective-permute-start.8 = (bf16[544,256]{1,0:T(8,128)(2,1)S(1)}, bf16[544,256]{1,0:T(8,128)(2,1)S(1)}, u32[]{:S(2)}, u32[]{:S(2)}) collective-permute-start(bf16[544,256]{1,0:T(8,128)(2,1)S(1)} %get-tuple-element.46), channel_id=1, source_target_pairs={{0,8},{1,9},{2,10},{3,11},{4,12},{5,13},{6,14},{7,15},{8,0},{9,1},... | collective-permute-start | bytes 835592 | tf_op jit(solution)/shard_map/ppermute | solution.py:40
  54.4 0.0 collective-permute-done.5
  54.4 0.0 collective-permute-done.6
  54.4 0.1 add_convert_fusion.1
  54.5 1.1 %collective-permute-start.7 = (bf16[544,256]{1,0:T(8,128)(2,1)S(1)}, bf16[544,256]{1,0:T(8,128)(2,1)S(1)}, u32[]{:S(2)}, u32[]{:S(2)}) collective-permute-start(bf16[544,256]{1,0:T(8,128)(2,1)S(1)} %add_convert_fusion.1), channel_id=1, source_target_pairs={{0,8},{1,9},{2,10},{3,11},{4,12},{5,13},{6,14},{7,15},{8,0},{9,1},... | collective-permute-start | bytes 835592 | tf_op jit(solution)/shard_map/ppermute | solution.py:40
  55.6 6.3 %collective-permute-done.8 = bf16[544,256]{1,0:T(8,128)(2,1)S(1)} collective-permute-done((bf16[544,256]{1,0:T(8,128)(2,1)S(1)}, bf16[544,256]{1,0:T(8,128)(2,1)S(1)}, u32[]{:S(2)}, u32[]{:S(2)}) %collective-permute-start.8) | collective-permute-done | bytes 278560 | tf_op jit(solution)/shard_map/ppermute | solution.py:40
  61.9 0.1 add_convert_fusion
  61.9 0.9 %collective-permute-start.9 = (bf16[544,256]{1,0:T(8,128)(2,1)S(1)}, bf16[544,256]{1,0:T(8,128)(2,1)S(1)}, u32[]{:S(2)}, u32[]{:S(2)}) collective-permute-start(bf16[544,256]{1,0:T(8,128)(2,1)S(1)} %add_convert_fusion), channel_id=1, source_target_pairs={{0,4},{1,5},{2,6},{3,7},{4,0},{5,1},{6,2},{7,3},{8,12},{9,13},{10,... | collective-permute-start | bytes 835592 | tf_op jit(solution)/shard_map/ppermute | solution.py:40
  62.9 0.0 collective-permute-done.2
  62.9 0.0 collective-permute-done.3
  62.9 3.9 %collective-permute-done.7 = bf16[544,256]{1,0:T(8,128)(2,1)S(1)} collective-permute-done((bf16[544,256]{1,0:T(8,128)(2,1)S(1)}, bf16[544,256]{1,0:T(8,128)(2,1)S(1)}, u32[]{:S(2)}, u32[]{:S(2)}) %collective-permute-start.7) | collective-permute-done | bytes 278560 | tf_op jit(solution)/shard_map/ppermute | solution.py:40
  66.8 0.1 convert_add_fusion.own_ref
  66.9 3.2 %collective-permute-done.9.far_ref = bf16[544,256]{1,0:T(8,128)(2,1)S(1)} collective-permute-done((bf16[544,256]{1,0:T(8,128)(2,1)S(1)}, bf16[544,256]{1,0:T(8,128)(2,1)S(1)}, u32[]{:S(2)}, u32[]{:S(2)}) %collective-permute-start.9) | collective-permute-done | bytes 278560 | tf_op jit(solution)/shard_map/ppermute | solution.py:40
  70.1 1.0 %shard_map.129 = (f32[256,512]{1,0:T(8,128)}, f32[32,256]{1,0:T(8,128)}) custom-call(f32[544,256]{1,0:T(8,128)S(1)} %convert_add_fusion.own_ref, bf16[544,256]{1,0:T(8,128)(2,1)S(1)} %collective-permute-done.9.far_ref), custom_call_target="tpu_custom_call" | custom-call | bytes 1048576 | tf_op jit(solution)/shard_map/pallas_call | solution.py:458
Async XLA Ops:
  0.6 24.7 %copy-start = (bf16[1,512,256]{2,1,0:T(8,128)(2,1)S(1)}, bf16[1,512,256]{2,1,0:T(8,128)(2,1)}, u32[]{:S(2)}) copy-start(bf16[1,512,256]{2,1,0:T(8,128)(2,1)} %param.19) | copy-start | bytes 786436
  0.6 24.6 %copy-start.1 = (s32[16,16]{1,0:T(8,128)S(1)}, s32[16,16]{1,0:T(8,128)}, u32[]{:S(2)}) copy-start(s32[16,16]{1,0:T(8,128)} %table_ref.1) | copy-start | bytes 3076
  0.7 24.6 %copy-start.2 = (s32[2048]{0:T(1024)S(1)}, s32[2048]{0:T(1024)}, u32[]{:S(2)}) copy-start(s32[2048]{0:T(1024)} %param.14) | copy-start | bytes 24580
  0.7 24.6 %copy-start.3 = (f32[2048]{0:T(1024)S(1)}, f32[2048]{0:T(1024)}, u32[]{:S(2)}) copy-start(f32[2048]{0:T(1024)} %param.15) | copy-start | bytes 24580
  0.7 24.6 %copy-start.4 = (s32[2048]{0:T(1024)S(1)}, s32[2048]{0:T(1024)}, u32[]{:S(2)}) copy-start(s32[2048]{0:T(1024)} %param.16) | copy-start | bytes 24580
  0.7 24.6 %copy-start.5 = (f32[2048]{0:T(1024)S(1)}, f32[2048]{0:T(1024)}, u32[]{:S(2)}) copy-start(f32[2048]{0:T(1024)} %param.17) | copy-start | bytes 24580
  31.7 2.8 %collective-permute-start.4 = (bf16[3,544,256]{2,1,0:T(8,128)(2,1)S(1)}, bf16[3,544,256]{2,1,0:T(8,128)(2,1)S(1)}, u32[]{:S(2)}, u32[]{:S(2)}) collective-permute-start(bf16[3,544,256]{2,1,0:T(8,128)(2,1)S(1)} %shard_map.127), channel_id=1, source_target_pairs={{0,1},{1,0},{2,3},{3,2},{4,5},{5,4},{6,7},{7,6},{8,9},{9,8},{10,11... | collective-permute-start | bytes 2506760 | tf_op jit(solution)/shard_map/ppermute | solution.py:40
  32.9 10.0 %collective-permute-start = (bf16[3,544,256]{2,1,0:T(8,128)(2,1)S(1)}, bf16[3,544,256]{2,1,0:T(8,128)(2,1)S(1)}, u32[]{:S(2)}, u32[]{:S(2)}) collective-permute-start(bf16[3,544,256]{2,1,0:T(8,128)(2,1)S(1)} %shard_map.123), channel_id=1, source_target_pairs={{0,1},{1,0},{2,3},{3,2},{4,5},{5,4},{6,7},{7,6},{8,9},{9,8},{10,11... | collective-permute-start | bytes 2506760 | tf_op jit(solution)/shard_map/ppermute | solution.py:40
  34.4 7.7 %collective-permute-start.1 = (bf16[2,544,256]{2,1,0:T(8,128)(2,1)S(1)}, bf16[2,544,256]{2,1,0:T(8,128)(2,1)S(1)}, u32[]{:S(2)}, u32[]{:S(2)}) collective-permute-start(bf16[2,544,256]{2,1,0:T(8,128)(2,1)S(1)} %shard_map.125), channel_id=1, source_target_pairs={{0,1},{1,0},{2,3},{3,2},{4,5},{5,4},{6,7},{7,6},{8,9},{9,8},{10,11... | collective-permute-start | bytes 1671176 | tf_op jit(solution)/shard_map/ppermute | solution.py:40
  35.8 18.5 %collective-permute-start.5 = (bf16[544,256]{1,0:T(8,128)(2,1)S(1)}, bf16[544,256]{1,0:T(8,128)(2,1)S(1)}, u32[]{:S(2)}, u32[]{:S(2)}) collective-permute-start(bf16[544,256]{1,0:T(8,128)(2,1)S(1)} %get-tuple-element.43), channel_id=1, source_target_pairs={{0,2},{1,3},{2,4},{3,5},{4,6},{5,7},{6,0},{7,1},{8,10},{9,11},{10,... | collective-permute-start | bytes 835592 | tf_op jit(solution)/shard_map/ppermute | solution.py:40
  39.0 15.4 %collective-permute-start.6 = (bf16[544,256]{1,0:T(8,128)(2,1)S(1)}, bf16[544,256]{1,0:T(8,128)(2,1)S(1)}, u32[]{:S(2)}, u32[]{:S(2)}) collective-permute-start(bf16[544,256]{1,0:T(8,128)(2,1)S(1)} %get-tuple-element.44), channel_id=1, source_target_pairs={{0,6},{1,7},{2,0},{3,1},{4,2},{5,3},{6,4},{7,5},{8,14},{9,15},{10,... | collective-permute-start | bytes 835592 | tf_op jit(solution)/shard_map/ppermute | solution.py:40
  44.4 18.4 %collective-permute-start.2 = (bf16[544,256]{1,0:T(8,128)(2,1)S(1)}, bf16[544,256]{1,0:T(8,128)(2,1)S(1)}, u32[]{:S(2)}, u32[]{:S(2)}) collective-permute-start(bf16[544,256]{1,0:T(8,128)(2,1)S(1)} %get-tuple-element.40), channel_id=1, source_target_pairs={{0,2},{1,3},{2,4},{3,5},{4,6},{5,7},{6,0},{7,1},{8,10},{9,11},{10,... | collective-permute-start | bytes 835592 | tf_op jit(solution)/shard_map/ppermute | solution.py:40
  44.5 18.4 %collective-permute-start.3 = (bf16[544,256]{1,0:T(8,128)(2,1)S(1)}, bf16[544,256]{1,0:T(8,128)(2,1)S(1)}, u32[]{:S(2)}, u32[]{:S(2)}) collective-permute-start(bf16[544,256]{1,0:T(8,128)(2,1)S(1)} %get-tuple-element.41), channel_id=1, source_target_pairs={{0,6},{1,7},{2,0},{3,1},{4,2},{5,3},{6,4},{7,5},{8,14},{9,15},{10,... | collective-permute-start | bytes 835592 | tf_op jit(solution)/shard_map/ppermute | solution.py:40
  47.7 14.1 %collective-permute-start.8 = (bf16[544,256]{1,0:T(8,128)(2,1)S(1)}, bf16[544,256]{1,0:T(8,128)(2,1)S(1)}, u32[]{:S(2)}, u32[]{:S(2)}) collective-permute-start(bf16[544,256]{1,0:T(8,128)(2,1)S(1)} %get-tuple-element.46), channel_id=1, source_target_pairs={{0,8},{1,9},{2,10},{3,11},{4,12},{5,13},{6,14},{7,15},{8,0},{9,1},... | collective-permute-start | bytes 835592 | tf_op jit(solution)/shard_map/ppermute | solution.py:40
  54.5 12.3 %collective-permute-start.7 = (bf16[544,256]{1,0:T(8,128)(2,1)S(1)}, bf16[544,256]{1,0:T(8,128)(2,1)S(1)}, u32[]{:S(2)}, u32[]{:S(2)}) collective-permute-start(bf16[544,256]{1,0:T(8,128)(2,1)S(1)} %add_convert_fusion.1), channel_id=1, source_target_pairs={{0,8},{1,9},{2,10},{3,11},{4,12},{5,13},{6,14},{7,15},{8,0},{9,1},... | collective-permute-start | bytes 835592 | tf_op jit(solution)/shard_map/ppermute | solution.py:40
  61.9 8.2 %collective-permute-start.9 = (bf16[544,256]{1,0:T(8,128)(2,1)S(1)}, bf16[544,256]{1,0:T(8,128)(2,1)S(1)}, u32[]{:S(2)}, u32[]{:S(2)}) collective-permute-start(bf16[544,256]{1,0:T(8,128)(2,1)S(1)} %add_convert_fusion), channel_id=1, source_target_pairs={{0,4},{1,5},{2,6},{3,7},{4,0},{5,1},{6,2},{7,3},{8,12},{9,13},{10,... | collective-permute-start | bytes 835592 | tf_op jit(solution)/shard_map/ppermute | solution.py:40

commit v3 on v2

--- a/solution.py
+++ b/solution.py
@@ -146,8 +146,8 @@
 
 def next_kernel(
     buffer_ref, w_in_ref, w_out_ref, fetch_ref, counts_ref, states_ref,
-    picked_ref, w_ref, first_ref, table_ref,
-    rows_ref, w_second, fetch, total, counts, table, sems, small_sems,
+    picked_ref, w_ref, first_ref, table,
+    rows_ref, w_second, fetch, total, counts, sems, small_sems,
 ):
     steps = sems.shape[1]
     depth = w_in_ref.shape[0] // steps
@@ -173,8 +173,6 @@
         table,
         lambda p: run_copy(table, states_ref, first_ref, small_sems.at[3], p).start(),
     )
-    kept_table = pltpu.make_async_copy(table, table_ref, small_sems.at[2])
-    kept_table.start()
     for i in range(steps):
         for copy in copies[i]:
             copy.wait()
@@ -197,24 +195,20 @@
         picked = jnp.where(rows < 128, found[0], found[1])
         for d in range(picked_ref.shape[0]):
             picked_ref[d, pl.ds(i, 8), :] = picked
-    kept_table.wait()
     gathered_block(states_ref, first_ref, small_sems.at[3]).wait()
 
 
 def member_kernel(
-    listed_ref, first_ref, states_ref, w_first, w_second, table_ref, best_ref,
+    table, first_ref, states_ref, w_first, w_second, table_ref, best_ref,
     actions_ref, rewards_ref, terminal_ref, returns_ref,
-    targets_ref, packed_ref, d_hidden_ref, grad_ref, blocks_ref,
-    raw, turned, slope, hidden_now, target_row, scale_row, act_row, table, sems, start_sems,
+    targets_ref, packed_ref, d_hidden_ref, grad_ref,
+    raw, turned, slope, hidden_now, target_row, scale_row, act_row, sems, start_sems,
 ):
     me = lax.axis_index("rep")
     owners, cap = rewards_ref.shape
-    load = pltpu.make_async_copy(listed_ref, table, start_sems.at[0])
-    load.start()
     place_first = pltpu.make_async_copy(
-        first_ref, packed_ref.at[pl.ds(0, BLOCK)], start_sems.at[1]
-    )
-    load.wait()
+        first_ref, packed_ref.at[pl.ds(0, BLOCK)], start_sems.at[0]
+    )
     blocks = table[1, owners]
 
     def fetch(b):
@@ -245,7 +239,6 @@
     for part in halves:
         raw[:, part] = jnp.dot(first_ref[...], w_first[:, part], preferred_element_type=F32)
         turn(part)
-    blocks_ref[...] = jnp.full(blocks_ref.shape, blocks, jnp.int32)
     counts = table_ref[...]
     counted = jnp.sum(counts).astype(F32)
     requester = lax.broadcasted_iota(jnp.int32, counts.shape, 1)
@@ -303,14 +296,15 @@
     place_first.wait()
 
 
-def piece_kernel(steps, parts, with_recv, blocks_ref, d_hidden_ref, states_ref, grad_ref, *rest):
+def piece_kernel(steps, parts, with_recv, table, d_hidden_ref, states_ref, grad_ref, *rest):
     recv_ref = rest[0] if with_recv else None
-    out_refs, total = rest[with_recv:-1], rest[-1]
+    out_refs, total = (rest[1:-1], rest[-1]) if with_recv else (rest, rest[-1])
     me = lax.axis_index("rep")
     y, x, core = me >> 3, (me >> 1) & 3, me & 1
-    blocks = blocks_ref[0, 0]
+    blocks = table[1, 16]
     width, depth = d_hidden_ref.shape[0], total.shape[2]
     rows = grad_ref.shape[0] // 16
+    first, second = pl.ds(0, width), pl.ds(width, rows)
     ats = [place(y ^ dy, (x + dx) & 3, core ^ dc) for dy, dx, dc in steps]
 
     for count in range(1, d_hidden_ref.shape[1] // BLOCK + 1):
@@ -322,21 +316,23 @@
                 for k in range(len(ats) - 1):
                     at = jnp.where(j == k, ats[k], at)
                 columns = pl.ds(pl.multiple_of(at * depth, depth), depth)
-                total[j, pl.ds(0, width), :] = jnp.dot(
+                term = jnp.dot(
                     d_hidden_ref[:, :deep], states_ref[:deep, columns], preferred_element_type=F32
                 )
+                if with_recv:
+                    term = term + high(recv_ref[j, first, :])
+                total[j, first, :] = term.astype(total.dtype)
                 return carry
 
             lax.fori_loop(0, len(ats), piece, 0)
 
     for j, at in enumerate(ats):
-        total[j, pl.ds(width, rows), :] = grad_ref[pl.ds(pl.multiple_of(at * rows, rows), rows), :]
-    if parts is None:
-        out_refs[0][...] = low(total[...])
-        return
-    for out, (j, first, last, _) in zip(out_refs, parts):
-        part = pl.ds(first, last - first)
-        out[...] = (total[j, part, :] + high(recv_ref[j, part, :])).astype(out.dtype)
+        term = grad_ref[pl.ds(pl.multiple_of(at * rows, rows), rows), :]
+        if with_recv:
+            term = term + high(recv_ref[j, second, :])
+        total[j, second, :] = term.astype(total.dtype)
+    for out, (j, start, stop, _) in zip(out_refs, parts or ()):
+        out[...] = total[j, pl.ds(start, stop - start), :].astype(out.dtype)
 
 
 def final_kernel(own_ref, far_ref, first_ref, second_ref):
@@ -362,7 +358,7 @@
             pltpu.VMEM((members, owners, cap), F32),
             pltpu.VMEM(w_first.shape, BF16),
             pltpu.VMEM((BLOCK, model), BF16),
-            pltpu.VMEM((8, slots // UNIT), jnp.int32),
+            pltpu.SMEM((8, slots // UNIT), jnp.int32),
         ],
         [HBM] * 6,
         [
@@ -371,12 +367,12 @@
             pltpu.VMEM((owners, cap), jnp.int32),
             pltpu.VMEM((buffer.shape[0], width), F32),
             pltpu.SMEM(fetch_counts.shape, jnp.int32),
-            pltpu.SMEM((8, slots // UNIT), jnp.int32),
             pltpu.SemaphoreType.DMA((2, 8)),
             pltpu.SemaphoreType.DMA((4,)),
         ],
         flops=2 * buffer.shape[0] * model * width,
         bytes_moved=6 << 20,
+        out_specs=[VMEM, VMEM, VMEM, SMEM],
     )(
         *[
             in_hbm(a)
@@ -387,22 +383,20 @@
         picked.reshape(members * owners, 1, cap), ("ens", "rep"), 0, 0, tiled=True
     ).reshape(members, owners, cap)
 
-    targets, packed, d_hidden, grad_second, blocks = call(
+    targets, packed, d_hidden, grad_second = call(
         member_kernel,
         [
             shape((owners, cap)),
             pltpu.VMEM((slots, model), BF16),
             pltpu.VMEM((width, slots), BF16),
             pltpu.VMEM((width, bins), F32),
-            pltpu.VMEM((8, 128), jnp.int32),
         ],
-        [VMEM, VMEM, HBM] + [VMEM] * 8,
+        [SMEM, VMEM, HBM] + [VMEM] * 8,
         [pltpu.VMEM((BLOCK, width), F32)]
         + [pltpu.VMEM((width, BLOCK), F32)] * 2
         + [pltpu.VMEM((width, BLOCK), BF16)]
         + [pltpu.VMEM((owners + 8, cap), F32)] * 3
-        + [pltpu.SMEM((8, slots // UNIT), jnp.int32)]
-        + [pltpu.SemaphoreType.DMA((slots // BLOCK,)), pltpu.SemaphoreType.DMA((2,))],
+        + [pltpu.SemaphoreType.DMA((slots // BLOCK,)), pltpu.SemaphoreType.DMA((1,))],
         flops=slots * model * width,
         bytes_moved=14 << 20,
     )(
@@ -424,11 +418,11 @@
         return call(
             functools.partial(piece_kernel, [(*s, core) for s in steps], parts, len(extra)),
             out,
-            [VMEM] * (4 + len(extra)),
-            [pltpu.VMEM((len(steps), tall, depth), F32)],
+            [SMEM] + [VMEM] * (3 + len(extra)),
+            [pltpu.VMEM((len(steps), tall, depth), F32)] if extra else [],
             flops=len(steps) * slots * width * depth,
             bytes_moved=len(steps) << 18,
-        )(blocks, d_hidden, packed, grad_second, *extra)
+        )(table, d_hidden, packed, grad_second, *extra)
 
     other = [(1, 2), (1, 1), (1, 3)]
     same = [(0, 2), (0, 1), (0, 3)]

time: 71.8 us -> 69.8 us (0.972)
  Pallas kernels: 16.7 us -> 15.2 us
    pallas_call x1, Pallas kernels: 5.34 us -> 4.58 us  [update(): call(member_kernel, [shape((owners, cap)), pltpu.VMEM((slots, model), BF1...]
    pallas_call x6, Pallas kernels: 6.42 us -> 5.69 us  [pieces(): call(functools.partial(piece_kernel, [(*s, core) for s in steps], parts,...]
  transfers between devices with their start and end apart: 10 -> 10, of which waited for: 3 -> 3; matrix products, arithmetic and copies ran while one was open for 0% -> 0% of each run, Pallas kernels for 8% -> 7%
where the time goes in v3:
time: 69.8 us; the launch traced here: 69 us
  blocking collectives  20.6 us (30%)
  starting transfers between devices  19 us (27%)
  Pallas kernels  15.2 us (22%)
  waiting for transfers between devices  13.1 us (19%)
  between operations  0.82 us (1%)
    all_to_all x1, blocking collectives, update(): lax.all_to_all(picked.reshape(members * owners, 1, cap), ('ens', 'rep'),...  20.6 us
    ppermute x10, starting transfers between devices, sent(): return lax.ppermute(value, 'rep', pairs)  19 us
    ppermute x10, waiting for transfers between devices, sent(): return lax.ppermute(value, 'rep', pairs)  13.1 us
    pallas_call x6, Pallas kernels, pieces(): call(functools.partial(piece_kernel, [(*s, core) for s in steps], parts,...  5.69 us
    pallas_call x1, Pallas kernels, update(): call(member_kernel, [shape((owners, cap)), pltpu.VMEM((slots, model), BF1...  4.58 us
    pallas_call x1, Pallas kernels, update(): call(next_kernel, [pltpu.VMEM((members, owners, cap), F32), pltpu.VMEM(w_...  3.92 us
  transfers between devices with their start and end apart: 10, of which 3 were waited for; matrix products, arithmetic and copies ran while one was open for 0% of the time, Pallas kernels for 7%

profile of v3, /device:TPU:0, one launch (start us, length us, event | category | flops | bytes accessed | tf_op | source)
XLA Modules:
  0.0 69.0 jit_solution(15602340531683300360)
XLA Ops:
  0.6 0.0 copy-start
  0.6 0.0 copy-start.1
  0.7 0.0 copy-start.2
  0.7 0.0 copy-start.3
  0.7 0.0 copy-start.4
  0.7 0.0 copy-start.5
  0.7 3.9 %shard_map.121 = (f32[8,16,128]{2,1,0:T(8,128)S(1)}, bf16[4096,512]{1,0:T(8,128)(2,1)S(1)}, bf16[256,4096]{1,0:T(8,128)(2,1)S(1)}, s32[8,128]{1,0:T(8,128)S(4)}) custom-call(bf16[256,4096]{1,0:T(8,128)(2,1)} %buffer_ref.1, bf16[4096,512]{1,0:T(8,128)(2,1)} %bitcast.22, bf16[512,256]{1,0:T(8,128)(2,1)} %bitcast.14, s32[16,128]{1,0:T(8,128)} %bitcast.23, ...), custom_call_target="tpu_custom_call" | custom-call | flops 1073741824 | bytes 6291456 | tf_op jit(solution)/shard_map/pallas_call | solution.py:355
  4.6 20.6 %all_to_all.5 = f32[128,1,128]{2,1,0:T(1,128)S(1)} all-to-all(f32[128,1,128]{2,1,0:T(1,128)S(1)} %bitcast.17), channel_id=1, replica_groups=mesh['ens'=8,'rep'=16] {'ens','rep'}, dimensions={0} | all-to-all | bytes 131072 | tf_op jit(solution)/shard_map/all_to_all | solution.py:382
  25.3 0.0 copy-done
  25.3 0.0 copy-done.1
  25.3 0.0 copy-done.2
  25.3 0.0 copy-done.3
  25.3 0.0 copy-done.4
  25.3 0.0 copy-done.5
  25.3 4.6 %shard_map.122 = (f32[16,128]{1,0:T(8,128)}, bf16[2048,4096]{1,0:T(8,128)(2,1)S(1)}, bf16[512,2048]{1,0:T(8,128)(2,1)S(1)}, f32[512,256]{1,0:T(8,128)S(1)}) custom-call(s32[8,128]{1,0:T(8,128)S(4)} %get-tuple-element.26.table, bf16[256,4096]{1,0:T(8,128)(2,1)S(1)} %get-tuple-element.27.first_ref, bf16[2048,4096]{1,0:T(8,128)(2,1)} %states_ref.3, ...), custom_call_target="tpu_custom_call" | custom-call | flops 4294967296 | bytes 14680064 | tf_op jit(solution)/shard_map/pallas_call | solution.py:386
  29.9 1.0 %shard_map.127 = bf16[3,544,256]{2,1,0:T(8,128)(2,1)S(1)} custom-call(s32[8,128]{1,0:T(8,128)S(4)} %get-tuple-element.26.table, bf16[512,2048]{1,0:T(8,128)(2,1)S(1)} %get-tuple-element.31.d_hidden_ref, bf16[2048,4096]{1,0:T(8,128)(2,1)S(1)} %get-tuple-element.32.states_ref, f32[512,256]{1,0:T(8,128)S(1)} %get-tuple-element.33.grad_ref), custom_call_target="tpu_custom_call" | custom-call | flops 805306368 | bytes 786432 | tf_op jit(solution)/shard_map/pallas_call | solution.py:418
  30.9 0.1 collective-permute-start.4
  31.0 1.0 %shard_map.123 = bf16[3,544,256]{2,1,0:T(8,128)(2,1)S(1)} custom-call(s32[8,128]{1,0:T(8,128)S(4)} %get-tuple-element.26.table, bf16[512,2048]{1,0:T(8,128)(2,1)S(1)} %get-tuple-element.31.d_hidden_ref, bf16[2048,4096]{1,0:T(8,128)(2,1)S(1)} %get-tuple-element.32.states_ref, f32[512,256]{1,0:T(8,128)S(1)} %get-tuple-element.33.grad_ref), custom_call_target="tpu_custom_call" | custom-call | flops 805306368 | bytes 786432 | tf_op jit(solution)/shard_map/pallas_call | solution.py:418
  32.0 0.5 collective-permute-start
  32.5 0.7 shard_map.125
  33.2 0.3 collective-permute-start.1
  33.5 0.0 collective-permute-done.4.rest_0_
  33.5 1.0 %shard_map.128 = (bf16[544,256]{1,0:T(8,128)(2,1)S(1)}, bf16[544,256]{1,0:T(8,128)(2,1)S(1)}, bf16[544,256]{1,0:T(8,128)(2,1)S(1)}) custom-call(s32[8,128]{1,0:T(8,128)S(4)} %get-tuple-element.26.table, bf16[512,2048]{1,0:T(8,128)(2,1)S(1)} %get-tuple-element.31.d_hidden_ref, bf16[2048,4096]{1,0:T(8,128)(2,1)S(1)} %get-tuple-element.32.states_ref, ...), custom_call_target="tpu_custom_call" | custom-call | flops 805306368 | bytes 786432 | tf_op jit(solution)/shard_map/pallas_call | solution.py:418
  34.5 3.0 %collective-permute-start.5 = (bf16[544,256]{1,0:T(8,128)(2,1)S(1)}, bf16[544,256]{1,0:T(8,128)(2,1)S(1)}, u32[]{:S(2)}, u32[]{:S(2)}) collective-permute-start(bf16[544,256]{1,0:T(8,128)(2,1)S(1)} %get-tuple-element.41), channel_id=1, source_target_pairs={{0,2},{1,3},{2,4},{3,5},{4,6},{5,7},{6,0},{7,1},{8,10},{9,11},{10,... | collective-permute-start | bytes 835592 | tf_op jit(solution)/shard_map/ppermute | solution.py:40
  37.6 2.9 %collective-permute-start.6 = (bf16[544,256]{1,0:T(8,128)(2,1)S(1)}, bf16[544,256]{1,0:T(8,128)(2,1)S(1)}, u32[]{:S(2)}, u32[]{:S(2)}) collective-permute-start(bf16[544,256]{1,0:T(8,128)(2,1)S(1)} %get-tuple-element.42), channel_id=1, source_target_pairs={{0,6},{1,7},{2,0},{3,1},{4,2},{5,3},{6,4},{7,5},{8,14},{9,15},{10,... | collective-permute-start | bytes 835592 | tf_op jit(solution)/shard_map/ppermute | solution.py:40
  40.5 0.0 collective-permute-done.1.rest_0_
  40.5 0.7 %shard_map.126 = (f32[544,256]{1,0:T(8,128)S(1)}, f32[544,256]{1,0:T(8,128)S(1)}) custom-call(s32[8,128]{1,0:T(8,128)S(4)} %get-tuple-element.26.table, bf16[512,2048]{1,0:T(8,128)(2,1)S(1)} %get-tuple-element.31.d_hidden_ref, bf16[2048,4096]{1,0:T(8,128)(2,1)S(1)} %get-tuple-element.32.states_ref, f32[512,256]{1,0:T(8,128)S(1)} %get-tuple-element.33.grad_ref, ...), custom_call_target="tpu_custom_call" | custom-call | flops 536870912 | bytes 524288 | tf_op jit(solution)/shard_map/pallas_call | solution.py:418
  41.2 0.0 collective-permute-done.rest_0_
  41.2 1.3 %shard_map.124 = (f32[544,256]{1,0:T(8,128)S(1)}, bf16[544,256]{1,0:T(8,128)(2,1)S(1)}, bf16[544,256]{1,0:T(8,128)(2,1)S(1)}) custom-call(s32[8,128]{1,0:T(8,128)S(4)} %get-tuple-element.26.table, bf16[512,2048]{1,0:T(8,128)(2,1)S(1)} %get-tuple-element.31.d_hidden_ref, bf16[2048,4096]{1,0:T(8,128)(2,1)S(1)} %get-tuple-element.32.states_ref, ...), custom_call_target="tpu_custom_call" | custom-call | flops 805306368 | bytes 786432 | tf_op jit(solution)/shard_map/pallas_call | solution.py:418
  42.5 0.1 collective-permute-start.2
  42.6 3.2 %collective-permute-start.3 = (bf16[544,256]{1,0:T(8,128)(2,1)S(1)}, bf16[544,256]{1,0:T(8,128)(2,1)S(1)}, u32[]{:S(2)}, u32[]{:S(2)}) collective-permute-start(bf16[544,256]{1,0:T(8,128)(2,1)S(1)} %get-tuple-element.39), channel_id=1, source_target_pairs={{0,6},{1,7},{2,0},{3,1},{4,2},{5,3},{6,4},{7,5},{8,14},{9,15},{10,... | collective-permute-start | bytes 835592 | tf_op jit(solution)/shard_map/ppermute | solution.py:40
  45.8 6.5 %collective-permute-start.8 = (bf16[544,256]{1,0:T(8,128)(2,1)S(1)}, bf16[544,256]{1,0:T(8,128)(2,1)S(1)}, u32[]{:S(2)}, u32[]{:S(2)}) collective-permute-start(bf16[544,256]{1,0:T(8,128)(2,1)S(1)} %get-tuple-element.44), channel_id=1, source_target_pairs={{0,8},{1,9},{2,10},{3,11},{4,12},{5,13},{6,14},{7,15},{8,0},{9,1},... | collective-permute-start | bytes 835592 | tf_op jit(solution)/shard_map/ppermute | solution.py:40
  52.3 0.0 collective-permute-done.5
  52.3 0.0 collective-permute-done.6
  52.3 0.1 add_convert_fusion.1
  52.4 1.4 %collective-permute-start.7 = (bf16[544,256]{1,0:T(8,128)(2,1)S(1)}, bf16[544,256]{1,0:T(8,128)(2,1)S(1)}, u32[]{:S(2)}, u32[]{:S(2)}) collective-permute-start(bf16[544,256]{1,0:T(8,128)(2,1)S(1)} %add_convert_fusion.1), channel_id=1, source_target_pairs={{0,8},{1,9},{2,10},{3,11},{4,12},{5,13},{6,14},{7,15},{8,0},{9,1},... | collective-permute-start | bytes 835592 | tf_op jit(solution)/shard_map/ppermute | solution.py:40
  53.9 6.0 %collective-permute-done.8 = bf16[544,256]{1,0:T(8,128)(2,1)S(1)} collective-permute-done((bf16[544,256]{1,0:T(8,128)(2,1)S(1)}, bf16[544,256]{1,0:T(8,128)(2,1)S(1)}, u32[]{:S(2)}, u32[]{:S(2)}) %collective-permute-start.8) | collective-permute-done | bytes 278560 | tf_op jit(solution)/shard_map/ppermute | solution.py:40
  59.8 0.1 add_convert_fusion
  59.9 0.9 %collective-permute-start.9 = (bf16[544,256]{1,0:T(8,128)(2,1)S(1)}, bf16[544,256]{1,0:T(8,128)(2,1)S(1)}, u32[]{:S(2)}, u32[]{:S(2)}) collective-permute-start(bf16[544,256]{1,0:T(8,128)(2,1)S(1)} %add_convert_fusion), channel_id=1, source_target_pairs={{0,4},{1,5},{2,6},{3,7},{4,0},{5,1},{6,2},{7,3},{8,12},{9,13},{10,... | collective-permute-start | bytes 835592 | tf_op jit(solution)/shard_map/ppermute | solution.py:40
  60.8 0.0 collective-permute-done.2
  60.8 0.0 collective-permute-done.3
  60.8 3.8 %collective-permute-done.7 = bf16[544,256]{1,0:T(8,128)(2,1)S(1)} collective-permute-done((bf16[544,256]{1,0:T(8,128)(2,1)S(1)}, bf16[544,256]{1,0:T(8,128)(2,1)S(1)}, u32[]{:S(2)}, u32[]{:S(2)}) %collective-permute-start.7) | collective-permute-done | bytes 278560 | tf_op jit(solution)/shard_map/ppermute | solution.py:40
  64.6 0.1 convert_add_fusion.own_ref
  64.7 3.3 %collective-permute-done.9.far_ref = bf16[544,256]{1,0:T(8,128)(2,1)S(1)} collective-permute-done((bf16[544,256]{1,0:T(8,128)(2,1)S(1)}, bf16[544,256]{1,0:T(8,128)(2,1)S(1)}, u32[]{:S(2)}, u32[]{:S(2)}) %collective-permute-start.9) | collective-permute-done | bytes 278560 | tf_op jit(solution)/shard_map/ppermute | solution.py:40
  68.0 1.0 %shard_map.129 = (f32[256,512]{1,0:T(8,128)}, f32[32,256]{1,0:T(8,128)}) custom-call(f32[544,256]{1,0:T(8,128)S(1)} %convert_add_fusion.own_ref, bf16[544,256]{1,0:T(8,128)(2,1)S(1)} %collective-permute-done.9.far_ref), custom_call_target="tpu_custom_call" | custom-call | bytes 1048576 | tf_op jit(solution)/shard_map/pallas_call | solution.py:452
Async XLA Ops:
  0.6 24.6 %copy-start = (bf16[1,512,256]{2,1,0:T(8,128)(2,1)S(1)}, bf16[1,512,256]{2,1,0:T(8,128)(2,1)}, u32[]{:S(2)}) copy-start(bf16[1,512,256]{2,1,0:T(8,128)(2,1)} %param.19) | copy-start | bytes 786436
  0.6 24.6 %copy-start.1 = (s32[16,16]{1,0:T(8,128)S(1)}, s32[16,16]{1,0:T(8,128)}, u32[]{:S(2)}) copy-start(s32[16,16]{1,0:T(8,128)} %table_ref.1) | copy-start | bytes 3076
  0.7 24.6 %copy-start.2 = (s32[2048]{0:T(1024)S(1)}, s32[2048]{0:T(1024)}, u32[]{:S(2)}) copy-start(s32[2048]{0:T(1024)} %param.14) | copy-start | bytes 24580
  0.7 24.6 %copy-start.3 = (f32[2048]{0:T(1024)S(1)}, f32[2048]{0:T(1024)}, u32[]{:S(2)}) copy-start(f32[2048]{0:T(1024)} %param.15) | copy-start | bytes 24580
  0.7 24.6 %copy-start.4 = (s32[2048]{0:T(1024)S(1)}, s32[2048]{0:T(1024)}, u32[]{:S(2)}) copy-start(s32[2048]{0:T(1024)} %param.16) | copy-start | bytes 24580
  0.7 24.6 %copy-start.5 = (f32[2048]{0:T(1024)S(1)}, f32[2048]{0:T(1024)}, u32[]{:S(2)}) copy-start(f32[2048]{0:T(1024)} %param.17) | copy-start | bytes 24580
  30.9 2.6 %collective-permute-start.4 = (bf16[3,544,256]{2,1,0:T(8,128)(2,1)S(1)}, bf16[3,544,256]{2,1,0:T(8,128)(2,1)S(1)}, u32[]{:S(2)}, u32[]{:S(2)}) collective-permute-start(bf16[3,544,256]{2,1,0:T(8,128)(2,1)S(1)} %shard_map.127), channel_id=1, source_target_pairs={{0,1},{1,0},{2,3},{3,2},{4,5},{5,4},{6,7},{7,6},{8,9},{9,8},{10,11... | collective-permute-start | bytes 2506760 | tf_op jit(solution)/shard_map/ppermute | solution.py:40
  32.0 9.2 %collective-permute-start = (bf16[3,544,256]{2,1,0:T(8,128)(2,1)S(1)}, bf16[3,544,256]{2,1,0:T(8,128)(2,1)S(1)}, u32[]{:S(2)}, u32[]{:S(2)}) collective-permute-start(bf16[3,544,256]{2,1,0:T(8,128)(2,1)S(1)} %shard_map.123), channel_id=1, source_target_pairs={{0,1},{1,0},{2,3},{3,2},{4,5},{5,4},{6,7},{7,6},{8,9},{9,8},{10,11... | collective-permute-start | bytes 2506760 | tf_op jit(solution)/shard_map/ppermute | solution.py:40
  33.2 7.3 %collective-permute-start.1 = (bf16[2,544,256]{2,1,0:T(8,128)(2,1)S(1)}, bf16[2,544,256]{2,1,0:T(8,128)(2,1)S(1)}, u32[]{:S(2)}, u32[]{:S(2)}) collective-permute-start(bf16[2,544,256]{2,1,0:T(8,128)(2,1)S(1)} %shard_map.125), channel_id=1, source_target_pairs={{0,1},{1,0},{2,3},{3,2},{4,5},{5,4},{6,7},{7,6},{8,9},{9,8},{10,11... | collective-permute-start | bytes 1671176 | tf_op jit(solution)/shard_map/ppermute | solution.py:40
  34.5 17.8 %collective-permute-start.5 = (bf16[544,256]{1,0:T(8,128)(2,1)S(1)}, bf16[544,256]{1,0:T(8,128)(2,1)S(1)}, u32[]{:S(2)}, u32[]{:S(2)}) collective-permute-start(bf16[544,256]{1,0:T(8,128)(2,1)S(1)} %get-tuple-element.41), channel_id=1, source_target_pairs={{0,2},{1,3},{2,4},{3,5},{4,6},{5,7},{6,0},{7,1},{8,10},{9,11},{10,... | collective-permute-start | bytes 835592 | tf_op jit(solution)/shard_map/ppermute | solution.py:40
  37.6 14.8 %collective-permute-start.6 = (bf16[544,256]{1,0:T(8,128)(2,1)S(1)}, bf16[544,256]{1,0:T(8,128)(2,1)S(1)}, u32[]{:S(2)}, u32[]{:S(2)}) collective-permute-start(bf16[544,256]{1,0:T(8,128)(2,1)S(1)} %get-tuple-element.42), channel_id=1, source_target_pairs={{0,6},{1,7},{2,0},{3,1},{4,2},{5,3},{6,4},{7,5},{8,14},{9,15},{10,... | collective-permute-start | bytes 835592 | tf_op jit(solution)/shard_map/ppermute | solution.py:40
  42.5 18.3 %collective-permute-start.2 = (bf16[544,256]{1,0:T(8,128)(2,1)S(1)}, bf16[544,256]{1,0:T(8,128)(2,1)S(1)}, u32[]{:S(2)}, u32[]{:S(2)}) collective-permute-start(bf16[544,256]{1,0:T(8,128)(2,1)S(1)} %get-tuple-element.38), channel_id=1, source_target_pairs={{0,2},{1,3},{2,4},{3,5},{4,6},{5,7},{6,0},{7,1},{8,10},{9,11},{10,... | collective-permute-start | bytes 835592 | tf_op jit(solution)/shard_map/ppermute | solution.py:40
  42.6 18.2 %collective-permute-start.3 = (bf16[544,256]{1,0:T(8,128)(2,1)S(1)}, bf16[544,256]{1,0:T(8,128)(2,1)S(1)}, u32[]{:S(2)}, u32[]{:S(2)}) collective-permute-start(bf16[544,256]{1,0:T(8,128)(2,1)S(1)} %get-tuple-element.39), channel_id=1, source_target_pairs={{0,6},{1,7},{2,0},{3,1},{4,2},{5,3},{6,4},{7,5},{8,14},{9,15},{10,... | collective-permute-start | bytes 835592 | tf_op jit(solution)/shard_map/ppermute | solution.py:40
  45.8 14.0 %collective-permute-start.8 = (bf16[544,256]{1,0:T(8,128)(2,1)S(1)}, bf16[544,256]{1,0:T(8,128)(2,1)S(1)}, u32[]{:S(2)}, u32[]{:S(2)}) collective-permute-start(bf16[544,256]{1,0:T(8,128)(2,1)S(1)} %get-tuple-element.44), channel_id=1, source_target_pairs={{0,8},{1,9},{2,10},{3,11},{4,12},{5,13},{6,14},{7,15},{8,0},{9,1},... | collective-permute-start | bytes 835592 | tf_op jit(solution)/shard_map/ppermute | solution.py:40
  52.4 12.1 %collective-permute-start.7 = (bf16[544,256]{1,0:T(8,128)(2,1)S(1)}, bf16[544,256]{1,0:T(8,128)(2,1)S(1)}, u32[]{:S(2)}, u32[]{:S(2)}) collective-permute-start(bf16[544,256]{1,0:T(8,128)(2,1)S(1)} %add_convert_fusion.1), channel_id=1, source_target_pairs={{0,8},{1,9},{2,10},{3,11},{4,12},{5,13},{6,14},{7,15},{8,0},{9,1},... | collective-permute-start | bytes 835592 | tf_op jit(solution)/shard_map/ppermute | solution.py:40
  59.9 8.1 %collective-permute-start.9 = (bf16[544,256]{1,0:T(8,128)(2,1)S(1)}, bf16[544,256]{1,0:T(8,128)(2,1)S(1)}, u32[]{:S(2)}, u32[]{:S(2)}) collective-permute-start(bf16[544,256]{1,0:T(8,128)(2,1)S(1)} %add_convert_fusion), channel_id=1, source_target_pairs={{0,4},{1,5},{2,6},{3,7},{4,0},{5,1},{6,2},{7,3},{8,12},{9,13},{10,... | collective-permute-start | bytes 835592 | tf_op jit(solution)/shard_map/ppermute | solution.py:40

commit v4 on v3

--- a/solution.py
+++ b/solution.py
@@ -220,8 +220,6 @@
                 ).start()
 
     fetch(jnp.int32(1))
-    fetch(jnp.int32(2))
-    place_first.start()
 
     def arrived(b):
         gathered_block(states_ref, packed_ref, sems.at[b]).wait()
@@ -291,12 +289,14 @@
         finish(b - 1, b)
         return carry
 
+    fetch(jnp.int32(2))
+    place_first.start()
     lax.fori_loop(1, blocks, step, 0)
     finish(blocks - 1)
     place_first.wait()
 
 
-def piece_kernel(steps, parts, with_recv, table, d_hidden_ref, states_ref, grad_ref, *rest):
+def piece_kernel(steps, parts, with_recv, skip, table, d_hidden_ref, states_ref, grad_ref, *rest):
     recv_ref = rest[0] if with_recv else None
     out_refs, total = (rest[1:-1], rest[-1]) if with_recv else (rest, rest[-1])
     me = lax.axis_index("rep")
@@ -320,7 +320,7 @@
                     d_hidden_ref[:, :deep], states_ref[:deep, columns], preferred_element_type=F32
                 )
                 if with_recv:
-                    term = term + high(recv_ref[j, first, :])
+                    term = term + high(recv_ref[j + skip, first, :])
                 total[j, first, :] = term.astype(total.dtype)
                 return carry
 
@@ -329,7 +329,7 @@
     for j, at in enumerate(ats):
         term = grad_ref[pl.ds(pl.multiple_of(at * rows, rows), rows), :]
         if with_recv:
-            term = term + high(recv_ref[j, second, :])
+            term = term + high(recv_ref[j + skip, second, :])
         total[j, second, :] = term.astype(total.dtype)
     for out, (j, start, stop, _) in zip(out_refs, parts or ()):
         out[...] = total[j, pl.ds(start, stop - start), :].astype(out.dtype)
@@ -407,7 +407,7 @@
     depth = model // 16
     tall = width + width // 16
 
-    def pieces(steps, parts=None, recv=None):
+    def pieces(steps, parts=None, recv=None, skip=0):
         out = (
             shape((len(steps), tall, depth), BF16)
             if parts is None
@@ -416,7 +416,7 @@
         extra = () if recv is None else (recv,)
         core = 0 if extra else 1
         return call(
-            functools.partial(piece_kernel, [(*s, core) for s in steps], parts, len(extra)),
+            functools.partial(piece_kernel, [(*s, core) for s in steps], parts, len(extra), skip),
             out,
             [SMEM] + [VMEM] * (3 + len(extra)),
             [pltpu.VMEM((len(steps), tall, depth), F32)] if extra else [],
@@ -424,25 +424,23 @@
             bytes_moved=len(steps) << 18,
         )(table, d_hidden, packed, grad_second, *extra)
 
-    other = [(1, 2), (1, 1), (1, 3)]
-    same = [(0, 2), (0, 1), (0, 3)]
-    own = [(1, 0), (0, 0)]
+    other = [(1, 1), (1, 3)]
+    middle = [(1, 2), (0, 1), (0, 3)]
+    last = [(0, 2), (1, 0), (0, 0)]
+    whole = lambda *dtypes: [(j, 0, tall, dtype) for j, dtype in enumerate(dtypes)]
 
     away_other = sent(pieces(other), CORE)
-    away_same = sent(pieces(same), CORE)
-    far_other, right_other, left_other = pieces(
-        other, [(j, 0, tall, BF16) for j in range(3)], away_other
-    )
-    across_far = sent(far_other, ACROSS)
+    away_middle = sent(pieces(middle), CORE)
+    right_other, left_other = pieces(other, whole(BF16, BF16), away_other)
     from_left_other = sent(right_other, RIGHT)
     from_right_other = sent(left_other, LEFT)
-    away_own = sent(pieces(own), CORE)
-    far_same, right_same, left_same = pieces(
-        same, [(j, 0, tall, dtype) for j, dtype in enumerate((F32, BF16, BF16))], away_same
-    )
+    (far_other,) = pieces(middle[:1], whole(BF16), away_middle)
+    across_far = sent(far_other, ACROSS)
+    away_last = sent(pieces(last), CORE)
+    right_same, left_same = pieces(middle[1:], whole(BF16, BF16), away_middle, 1)
     from_left_same = sent(right_same, RIGHT)
     from_right_same = sent(left_same, LEFT)
-    own_other, own_same = pieces(own, [(j, 0, tall, F32) for j in range(2)], away_own)
+    far_same, own_other, own_same = pieces(last, whole(F32, F32, F32), away_last)
     far_same, own_other, own_same = after(far_same, own_other, own_same)
     from_far = sent(low(far_same + high(across_far)), FAR)
     own_other = own_other + high(from_left_other) + high(from_right_other)

time: 69.8 us -> 71.5 us (1.024)
  waiting for transfers between devices: 13.1 us -> 15.5 us
    ppermute x10, waiting for transfers between devices: 13.1 us -> 15.5 us  [sent(): return lax.ppermute(value, 'rep', pairs)]
    ppermute x10, starting transfers between devices: 19 us -> 18.3 us  [sent(): return lax.ppermute(value, 'rep', pairs)]
    pallas_call x6 -> x7, Pallas kernels: 5.69 us -> 5.71 us  [pieces(): call(functools.partial(piece_kernel, [(*s, core) for s in steps], parts,...]
  transfers between devices with their start and end apart: 10 -> 10, of which waited for: 3 -> 4; matrix products, arithmetic and copies ran while one was open for 0% -> 0% of each run, Pallas kernels for 7% -> 7%
where the time goes in v4:
time: 71.5 us; the launch traced here: 70.7 us
  blocking collectives  20.6 us (29%)
  starting transfers between devices  18.3 us (26%)
  waiting for transfers between devices  15.5 us (22%)
  Pallas kernels  15.2 us (21%)
  between operations  0.83 us (1%)
    all_to_all x1, blocking collectives, update(): lax.all_to_all(picked.reshape(members * owners, 1, cap), ('ens', 'rep'),...  20.6 us
    ppermute x10, starting transfers between devices, sent(): return lax.ppermute(value, 'rep', pairs)  18.3 us
    ppermute x10, waiting for transfers between devices, sent(): return lax.ppermute(value, 'rep', pairs)  15.5 us
    pallas_call x7, Pallas kernels, pieces(): call(functools.partial(piece_kernel, [(*s, core) for s in steps], parts,...  5.71 us
    pallas_call x1, Pallas kernels, update(): call(member_kernel, [shape((owners, cap)), pltpu.VMEM((slots, model), BF1...  4.59 us
    pallas_call x1, Pallas kernels, update(): call(next_kernel, [pltpu.VMEM((members, owners, cap), F32), pltpu.VMEM(w_...  3.92 us
  transfers between devices with their start and end apart: 10, of which 4 were waited for; matrix products, arithmetic and copies ran while one was open for 0% of the time, Pallas kernels for 7%

profile of v4, /device:TPU:0, one launch (start us, length us, event | category | flops | bytes accessed | tf_op | source)
XLA Modules:
  0.0 70.7 jit_solution(16702920028947337884)
XLA Ops:
  0.6 0.0 copy-start
  0.6 0.0 copy-start.1
  0.7 0.0 copy-start.2
  0.7 0.0 copy-start.3
  0.7 0.0 copy-start.4
  0.7 0.0 copy-start.5
  0.7 3.9 %shard_map.121 = (f32[8,16,128]{2,1,0:T(8,128)S(1)}, bf16[4096,512]{1,0:T(8,128)(2,1)S(1)}, bf16[256,4096]{1,0:T(8,128)(2,1)S(1)}, s32[8,128]{1,0:T(8,128)S(4)}) custom-call(bf16[256,4096]{1,0:T(8,128)(2,1)} %buffer_ref.1, bf16[4096,512]{1,0:T(8,128)(2,1)} %bitcast.22, bf16[512,256]{1,0:T(8,128)(2,1)} %bitcast.14, s32[16,128]{1,0:T(8,128)} %bitcast.23, ...), custom_call_target="tpu_custom_call" | custom-call | flops 1073741824 | bytes 6291456 | tf_op jit(solution)/shard_map/pallas_call | solution.py:355
  4.6 20.6 %all_to_all.5 = f32[128,1,128]{2,1,0:T(1,128)S(1)} all-to-all(f32[128,1,128]{2,1,0:T(1,128)S(1)} %bitcast.17), channel_id=1, replica_groups=mesh['ens'=8,'rep'=16] {'ens','rep'}, dimensions={0} | all-to-all | bytes 131072 | tf_op jit(solution)/shard_map/all_to_all | solution.py:382
  25.3 0.0 copy-done
  25.3 0.0 copy-done.1
  25.3 0.0 copy-done.2
  25.3 0.0 copy-done.3
  25.3 0.0 copy-done.4
  25.3 0.0 copy-done.5
  25.3 4.6 %shard_map.122 = (f32[16,128]{1,0:T(8,128)}, bf16[2048,4096]{1,0:T(8,128)(2,1)S(1)}, bf16[512,2048]{1,0:T(8,128)(2,1)S(1)}, f32[512,256]{1,0:T(8,128)S(1)}) custom-call(s32[8,128]{1,0:T(8,128)S(4)} %get-tuple-element.22.table, bf16[256,4096]{1,0:T(8,128)(2,1)S(1)} %get-tuple-element.23.first_ref, bf16[2048,4096]{1,0:T(8,128)(2,1)} %states_ref.3, ...), custom_call_target="tpu_custom_call" | custom-call | flops 4294967296 | bytes 14680064 | tf_op jit(solution)/shard_map/pallas_call | solution.py:386
  29.9 1.0 %shard_map.123 = bf16[3,544,256]{2,1,0:T(8,128)(2,1)S(1)} custom-call(s32[8,128]{1,0:T(8,128)S(4)} %get-tuple-element.22.table, bf16[512,2048]{1,0:T(8,128)(2,1)S(1)} %get-tuple-element.27.d_hidden_ref, bf16[2048,4096]{1,0:T(8,128)(2,1)S(1)} %get-tuple-element.28.states_ref, f32[512,256]{1,0:T(8,128)S(1)} %get-tuple-element.29.grad_ref), custom_call_target="tpu_custom_call" | custom-call | flops 805306368 | bytes 786432 | tf_op jit(solution)/shard_map/pallas_call | solution.py:418
  30.9 0.1 collective-permute-start
  31.0 1.0 %shard_map.125 = bf16[3,544,256]{2,1,0:T(8,128)(2,1)S(1)} custom-call(s32[8,128]{1,0:T(8,128)S(4)} %get-tuple-element.22.table, bf16[512,2048]{1,0:T(8,128)(2,1)S(1)} %get-tuple-element.27.d_hidden_ref, bf16[2048,4096]{1,0:T(8,128)(2,1)S(1)} %get-tuple-element.28.states_ref, f32[512,256]{1,0:T(8,128)S(1)} %get-tuple-element.29.grad_ref), custom_call_target="tpu_custom_call" | custom-call | flops 805306368 | bytes 786432 | tf_op jit(solution)/shard_map/pallas_call | solution.py:418
  32.0 0.5 collective-permute-start.1
  32.5 0.7 shard_map.127
  33.2 0.3 collective-permute-start.4
  33.5 1.8 %collective-permute-done.4.rest_0_ = bf16[2,544,256]{2,1,0:T(8,128)(2,1)S(1)} collective-permute-done((bf16[2,544,256]{2,1,0:T(8,128)(2,1)S(1)}, bf16[2,544,256]{2,1,0:T(8,128)(2,1)S(1)}, u32[]{:S(2)}, u32[]{:S(2)}) %collective-permute-start.4) | collective-permute-done | bytes 557088 | tf_op jit(solution)/shard_map/ppermute | solution.py:40
  35.3 0.7 shard_map.128
  36.0 2.8 %collective-permute-start.5 = (bf16[544,256]{1,0:T(8,128)(2,1)S(1)}, bf16[544,256]{1,0:T(8,128)(2,1)S(1)}, u32[]{:S(2)}, u32[]{:S(2)}) collective-permute-start(bf16[544,256]{1,0:T(8,128)(2,1)S(1)} %get-tuple-element.34), channel_id=1, source_target_pairs={{0,2},{1,3},{2,4},{3,5},{4,6},{5,7},{6,0},{7,1},{8,10},{9,11},{10,... | collective-permute-start | bytes 835592 | tf_op jit(solution)/shard_map/ppermute | solution.py:40
  38.8 3.0 %collective-permute-start.6 = (bf16[544,256]{1,0:T(8,128)(2,1)S(1)}, bf16[544,256]{1,0:T(8,128)(2,1)S(1)}, u32[]{:S(2)}, u32[]{:S(2)}) collective-permute-start(bf16[544,256]{1,0:T(8,128)(2,1)S(1)} %get-tuple-element.35), channel_id=1, source_target_pairs={{0,6},{1,7},{2,0},{3,1},{4,2},{5,3},{6,4},{7,5},{8,14},{9,15},{10,... | collective-permute-start | bytes 835592 | tf_op jit(solution)/shard_map/ppermute | solution.py:40
  41.8 0.0 collective-permute-done.rest_0_
  41.8 1.1 %shard_map.124 = (f32[544,256]{1,0:T(8,128)S(1)}, f32[544,256]{1,0:T(8,128)S(1)}, f32[544,256]{1,0:T(8,128)S(1)}) custom-call(s32[8,128]{1,0:T(8,128)S(4)} %get-tuple-element.22.table, bf16[512,2048]{1,0:T(8,128)(2,1)S(1)} %get-tuple-element.27.d_hidden_ref, bf16[2048,4096]{1,0:T(8,128)(2,1)S(1)} %get-tuple-element.28.states_ref, ...), custom_call_target="tpu_custom_call" | custom-call | flops 805306368 | bytes 786432 | tf_op jit(solution)/shard_map/pallas_call | solution.py:418
  42.9 0.0 collective-permute-done.1.rest_0_
  42.9 0.9 %shard_map.126 = (bf16[544,256]{1,0:T(8,128)(2,1)S(1)}, bf16[544,256]{1,0:T(8,128)(2,1)S(1)}) custom-call(s32[8,128]{1,0:T(8,128)S(4)} %get-tuple-element.22.table, bf16[512,2048]{1,0:T(8,128)(2,1)S(1)} %get-tuple-element.27.d_hidden_ref, bf16[2048,4096]{1,0:T(8,128)(2,1)S(1)} %get-tuple-element.28.states_ref, f32[512,256]{1,0:T(8,128)S(1)} %get-tuple-element.29.grad_ref, ...), custom_call_target="tpu_custom_call" | custom-call | flops 536870912 | bytes 524288 | tf_op jit(solution)/shard_map/pallas_call | solution.py:418
  43.8 0.1 collective-permute-start.2
  43.9 3.2 %collective-permute-start.3 = (bf16[544,256]{1,0:T(8,128)(2,1)S(1)}, bf16[544,256]{1,0:T(8,128)(2,1)S(1)}, u32[]{:S(2)}, u32[]{:S(2)}) collective-permute-start(bf16[544,256]{1,0:T(8,128)(2,1)S(1)} %get-tuple-element.32), channel_id=1, source_target_pairs={{0,6},{1,7},{2,0},{3,1},{4,2},{5,3},{6,4},{7,5},{8,14},{9,15},{10,... | collective-permute-start | bytes 835592 | tf_op jit(solution)/shard_map/ppermute | solution.py:40
  47.1 0.4 shard_map.129
  47.5 6.5 %collective-permute-start.8 = (bf16[544,256]{1,0:T(8,128)(2,1)S(1)}, bf16[544,256]{1,0:T(8,128)(2,1)S(1)}, u32[]{:S(2)}, u32[]{:S(2)}) collective-permute-start(bf16[544,256]{1,0:T(8,128)(2,1)S(1)} %shard_map.129), channel_id=1, source_target_pairs={{0,8},{1,9},{2,10},{3,11},{4,12},{5,13},{6,14},{7,15},{8,0},{9,1},... | collective-permute-start | bytes 835592 | tf_op jit(solution)/shard_map/ppermute | solution.py:40
  54.0 0.0 collective-permute-done.5
  54.0 0.0 collective-permute-done.6
  54.0 0.1 add_convert_fusion.1
  54.1 0.8 %collective-permute-start.7 = (bf16[544,256]{1,0:T(8,128)(2,1)S(1)}, bf16[544,256]{1,0:T(8,128)(2,1)S(1)}, u32[]{:S(2)}, u32[]{:S(2)}) collective-permute-start(bf16[544,256]{1,0:T(8,128)(2,1)S(1)} %add_convert_fusion.1), channel_id=1, source_target_pairs={{0,8},{1,9},{2,10},{3,11},{4,12},{5,13},{6,14},{7,15},{8,0},{9,1},... | collective-permute-start | bytes 835592 | tf_op jit(solution)/shard_map/ppermute | solution.py:40
  54.9 6.6 %collective-permute-done.8 = bf16[544,256]{1,0:T(8,128)(2,1)S(1)} collective-permute-done((bf16[544,256]{1,0:T(8,128)(2,1)S(1)}, bf16[544,256]{1,0:T(8,128)(2,1)S(1)}, u32[]{:S(2)}, u32[]{:S(2)}) %collective-permute-start.8) | collective-permute-done | bytes 278560 | tf_op jit(solution)/shard_map/ppermute | solution.py:40
  61.5 0.1 add_convert_fusion
  61.6 1.0 %collective-permute-start.9 = (bf16[544,256]{1,0:T(8,128)(2,1)S(1)}, bf16[544,256]{1,0:T(8,128)(2,1)S(1)}, u32[]{:S(2)}, u32[]{:S(2)}) collective-permute-start(bf16[544,256]{1,0:T(8,128)(2,1)S(1)} %add_convert_fusion), channel_id=1, source_target_pairs={{0,4},{1,5},{2,6},{3,7},{4,0},{5,1},{6,2},{7,3},{8,12},{9,13},{10,... | collective-permute-start | bytes 835592 | tf_op jit(solution)/shard_map/ppermute | solution.py:40
  62.6 0.0 collective-permute-done.2
  62.6 0.0 collective-permute-done.3
  62.6 3.6 %collective-permute-done.7 = bf16[544,256]{1,0:T(8,128)(2,1)S(1)} collective-permute-done((bf16[544,256]{1,0:T(8,128)(2,1)S(1)}, bf16[544,256]{1,0:T(8,128)(2,1)S(1)}, u32[]{:S(2)}, u32[]{:S(2)}) %collective-permute-start.7) | collective-permute-done | bytes 278560 | tf_op jit(solution)/shard_map/ppermute | solution.py:40
  66.2 0.1 convert_add_fusion.own_ref
  66.3 3.4 %collective-permute-done.9.far_ref = bf16[544,256]{1,0:T(8,128)(2,1)S(1)} collective-permute-done((bf16[544,256]{1,0:T(8,128)(2,1)S(1)}, bf16[544,256]{1,0:T(8,128)(2,1)S(1)}, u32[]{:S(2)}, u32[]{:S(2)}) %collective-permute-start.9) | collective-permute-done | bytes 278560 | tf_op jit(solution)/shard_map/ppermute | solution.py:40
  69.7 1.0 %shard_map.130 = (f32[256,512]{1,0:T(8,128)}, f32[32,256]{1,0:T(8,128)}) custom-call(f32[544,256]{1,0:T(8,128)S(1)} %convert_add_fusion.own_ref, bf16[544,256]{1,0:T(8,128)(2,1)S(1)} %collective-permute-done.9.far_ref), custom_call_target="tpu_custom_call" | custom-call | bytes 1048576 | tf_op jit(solution)/shard_map/pallas_call | solution.py:450
Async XLA Ops:
  0.6 24.6 %copy-start = (bf16[1,512,256]{2,1,0:T(8,128)(2,1)S(1)}, bf16[1,512,256]{2,1,0:T(8,128)(2,1)}, u32[]{:S(2)}) copy-start(bf16[1,512,256]{2,1,0:T(8,128)(2,1)} %param.19) | copy-start | bytes 786436
  0.6 24.6 %copy-start.1 = (s32[16,16]{1,0:T(8,128)S(1)}, s32[16,16]{1,0:T(8,128)}, u32[]{:S(2)}) copy-start(s32[16,16]{1,0:T(8,128)} %table_ref.1) | copy-start | bytes 3076
  0.7 24.6 %copy-start.2 = (s32[2048]{0:T(1024)S(1)}, s32[2048]{0:T(1024)}, u32[]{:S(2)}) copy-start(s32[2048]{0:T(1024)} %param.14) | copy-start | bytes 24580
  0.7 24.6 %copy-start.3 = (f32[2048]{0:T(1024)S(1)}, f32[2048]{0:T(1024)}, u32[]{:S(2)}) copy-start(f32[2048]{0:T(1024)} %param.15) | copy-start | bytes 24580
  0.7 24.6 %copy-start.4 = (s32[2048]{0:T(1024)S(1)}, s32[2048]{0:T(1024)}, u32[]{:S(2)}) copy-start(s32[2048]{0:T(1024)} %param.16) | copy-start | bytes 24580
  0.7 24.6 %copy-start.5 = (f32[2048]{0:T(1024)S(1)}, f32[2048]{0:T(1024)}, u32[]{:S(2)}) copy-start(f32[2048]{0:T(1024)} %param.17) | copy-start | bytes 24580
  30.9 10.9 %collective-permute-start = (bf16[3,544,256]{2,1,0:T(8,128)(2,1)S(1)}, bf16[3,544,256]{2,1,0:T(8,128)(2,1)S(1)}, u32[]{:S(2)}, u32[]{:S(2)}) collective-permute-start(bf16[3,544,256]{2,1,0:T(8,128)(2,1)S(1)} %shard_map.123), channel_id=1, source_target_pairs={{0,1},{1,0},{2,3},{3,2},{4,5},{5,4},{6,7},{7,6},{8,9},{9,8},{10,11... | collective-permute-start | bytes 2506760 | tf_op jit(solution)/shard_map/ppermute | solution.py:40
  32.0 10.9 %collective-permute-start.1 = (bf16[3,544,256]{2,1,0:T(8,128)(2,1)S(1)}, bf16[3,544,256]{2,1,0:T(8,128)(2,1)S(1)}, u32[]{:S(2)}, u32[]{:S(2)}) collective-permute-start(bf16[3,544,256]{2,1,0:T(8,128)(2,1)S(1)} %shard_map.125), channel_id=1, source_target_pairs={{0,1},{1,0},{2,3},{3,2},{4,5},{5,4},{6,7},{7,6},{8,9},{9,8},{10,11... | collective-permute-start | bytes 2506760 | tf_op jit(solution)/shard_map/ppermute | solution.py:40
  33.2 2.1 %collective-permute-start.4 = (bf16[2,544,256]{2,1,0:T(8,128)(2,1)S(1)}, bf16[2,544,256]{2,1,0:T(8,128)(2,1)S(1)}, u32[]{:S(2)}, u32[]{:S(2)}) collective-permute-start(bf16[2,544,256]{2,1,0:T(8,128)(2,1)S(1)} %shard_map.127), channel_id=1, source_target_pairs={{0,1},{1,0},{2,3},{3,2},{4,5},{5,4},{6,7},{7,6},{8,9},{9,8},{10,11... | collective-permute-start | bytes 1671176 | tf_op jit(solution)/shard_map/ppermute | solution.py:40
  36.0 18.0 %collective-permute-start.5 = (bf16[544,256]{1,0:T(8,128)(2,1)S(1)}, bf16[544,256]{1,0:T(8,128)(2,1)S(1)}, u32[]{:S(2)}, u32[]{:S(2)}) collective-permute-start(bf16[544,256]{1,0:T(8,128)(2,1)S(1)} %get-tuple-element.34), channel_id=1, source_target_pairs={{0,2},{1,3},{2,4},{3,5},{4,6},{5,7},{6,0},{7,1},{8,10},{9,11},{10,... | collective-permute-start | bytes 835592 | tf_op jit(solution)/shard_map/ppermute | solution.py:40
  38.8 15.2 %collective-permute-start.6 = (bf16[544,256]{1,0:T(8,128)(2,1)S(1)}, bf16[544,256]{1,0:T(8,128)(2,1)S(1)}, u32[]{:S(2)}, u32[]{:S(2)}) collective-permute-start(bf16[544,256]{1,0:T(8,128)(2,1)S(1)} %get-tuple-element.35), channel_id=1, source_target_pairs={{0,6},{1,7},{2,0},{3,1},{4,2},{5,3},{6,4},{7,5},{8,14},{9,15},{10,... | collective-permute-start | bytes 835592 | tf_op jit(solution)/shard_map/ppermute | solution.py:40
  43.8 18.7 %collective-permute-start.2 = (bf16[544,256]{1,0:T(8,128)(2,1)S(1)}, bf16[544,256]{1,0:T(8,128)(2,1)S(1)}, u32[]{:S(2)}, u32[]{:S(2)}) collective-permute-start(bf16[544,256]{1,0:T(8,128)(2,1)S(1)} %get-tuple-element.31), channel_id=1, source_target_pairs={{0,2},{1,3},{2,4},{3,5},{4,6},{5,7},{6,0},{7,1},{8,10},{9,11},{10,... | collective-permute-start | bytes 835592 | tf_op jit(solution)/shard_map/ppermute | solution.py:40
  43.9 18.7 %collective-permute-start.3 = (bf16[544,256]{1,0:T(8,128)(2,1)S(1)}, bf16[544,256]{1,0:T(8,128)(2,1)S(1)}, u32[]{:S(2)}, u32[]{:S(2)}) collective-permute-start(bf16[544,256]{1,0:T(8,128)(2,1)S(1)} %get-tuple-element.32), channel_id=1, source_target_pairs={{0,6},{1,7},{2,0},{3,1},{4,2},{5,3},{6,4},{7,5},{8,14},{9,15},{10,... | collective-permute-start | bytes 835592 | tf_op jit(solution)/shard_map/ppermute | solution.py:40
  47.5 14.0 %collective-permute-start.8 = (bf16[544,256]{1,0:T(8,128)(2,1)S(1)}, bf16[544,256]{1,0:T(8,128)(2,1)S(1)}, u32[]{:S(2)}, u32[]{:S(2)}) collective-permute-start(bf16[544,256]{1,0:T(8,128)(2,1)S(1)} %shard_map.129), channel_id=1, source_target_pairs={{0,8},{1,9},{2,10},{3,11},{4,12},{5,13},{6,14},{7,15},{8,0},{9,1},... | collective-permute-start | bytes 835592 | tf_op jit(solution)/shard_map/ppermute | solution.py:40
  54.1 12.1 %collective-permute-start.7 = (bf16[544,256]{1,0:T(8,128)(2,1)S(1)}, bf16[544,256]{1,0:T(8,128)(2,1)S(1)}, u32[]{:S(2)}, u32[]{:S(2)}) collective-permute-start(bf16[544,256]{1,0:T(8,128)(2,1)S(1)} %add_convert_fusion.1), channel_id=1, source_target_pairs={{0,8},{1,9},{2,10},{3,11},{4,12},{5,13},{6,14},{7,15},{8,0},{9,1},... | collective-permute-start | bytes 835592 | tf_op jit(solution)/shard_map/ppermute | solution.py:40
  61.6 8.1 %collective-permute-start.9 = (bf16[544,256]{1,0:T(8,128)(2,1)S(1)}, bf16[544,256]{1,0:T(8,128)(2,1)S(1)}, u32[]{:S(2)}, u32[]{:S(2)}) collective-permute-start(bf16[544,256]{1,0:T(8,128)(2,1)S(1)} %add_convert_fusion), channel_id=1, source_target_pairs={{0,4},{1,5},{2,6},{3,7},{4,0},{5,1},{6,2},{7,3},{8,12},{9,13},{10,... | collective-permute-start | bytes 835592 | tf_op jit(solution)/shard_map/ppermute | solution.py:40

commit v5 on v4

--- a/solution.py
+++ b/solution.py
@@ -94,7 +94,7 @@
     )
 
 
-def listed(counts, table, start_first):
+def listed(counts, table):
     me = lax.axis_index("rep")
     owners = counts.shape[0]
     runs = table.shape[1] // owners
@@ -102,10 +102,6 @@
 
     def put(source, position):
         table[0, position] = source
-
-        @pl.when(position < per_block)
-        def _():
-            start_first(position)
 
     def owner(o, position):
         count = counts[o, me]
@@ -168,14 +164,13 @@
     second.start()
     wanted.start()
     counted.wait()
-    listed(
-        counts,
-        table,
-        lambda p: run_copy(table, states_ref, first_ref, small_sems.at[3], p).start(),
-    )
+    listed(counts, table)
     for i in range(steps):
         for copy in copies[i]:
             copy.wait()
+        if i == steps // 2:
+            for p in range(BLOCK // UNIT):
+                run_copy(table, states_ref, first_ref, small_sems.at[3], p).start()
         part = pl.ds(i * depth, depth)
         term = jnp.dot(rows_ref[:, part], w_ref[part, :], preferred_element_type=F32)
         total[...] = term if i == 0 else total[...] + term

time: 71.5 us -> 71.5 us (level)
  no operation moved by 1% of the time
where the time goes in v5:
time: 71.5 us; the launch traced here: 70.7 us
  blocking collectives  20.6 us (29%)
  starting transfers between devices  18.2 us (25%)
  waiting for transfers between devices  15.5 us (22%)
  Pallas kernels  15.3 us (21%)
  between operations  0.83 us (1%)
    all_to_all x1, blocking collectives, update(): lax.all_to_all(picked.reshape(members * owners, 1, cap), ('ens', 'rep'),...  20.6 us
    ppermute x10, starting transfers between devices, sent(): return lax.ppermute(value, 'rep', pairs)  18.2 us
    ppermute x10, waiting for transfers between devices, sent(): return lax.ppermute(value, 'rep', pairs)  15.5 us
    pallas_call x7, Pallas kernels, pieces(): call(functools.partial(piece_kernel, [(*s, core) for s in steps], parts,...  5.72 us
    pallas_call x1, Pallas kernels, update(): call(member_kernel, [shape((owners, cap)), pltpu.VMEM((slots, model), BF1...  4.59 us
    pallas_call x1, Pallas kernels, update(): call(next_kernel, [pltpu.VMEM((members, owners, cap), F32), pltpu.VMEM(w_...  4 us
  transfers between devices with their start and end apart: 10, of which 4 were waited for; matrix products, arithmetic and copies ran while one was open for 0% of the time, Pallas kernels for 7%

profile of v5, /device:TPU:0, one launch (start us, length us, event | category | flops | bytes accessed | tf_op | source)
XLA Modules:
  0.0 70.7 jit_solution(13572642187562287891)
XLA Ops:
  0.6 0.0 copy-start
  0.6 0.0 copy-start.1
  0.7 0.0 copy-start.2
  0.7 0.0 copy-start.3
  0.7 0.0 copy-start.4
  0.7 0.0 copy-start.5
  0.7 4.0 %shard_map.121 = (f32[8,16,128]{2,1,0:T(8,128)S(1)}, bf16[4096,512]{1,0:T(8,128)(2,1)S(1)}, bf16[256,4096]{1,0:T(8,128)(2,1)S(1)}, s32[8,128]{1,0:T(8,128)S(4)}) custom-call(bf16[256,4096]{1,0:T(8,128)(2,1)} %buffer_ref.1, bf16[4096,512]{1,0:T(8,128)(2,1)} %bitcast.22, bf16[512,256]{1,0:T(8,128)(2,1)} %bitcast.14, s32[16,128]{1,0:T(8,128)} %bitcast.23, ...), custom_call_target="tpu_custom_call" | custom-call | flops 1073741824 | bytes 6291456 | tf_op jit(solution)/shard_map/pallas_call | solution.py:350
  4.7 20.6 %all_to_all.5 = f32[128,1,128]{2,1,0:T(1,128)S(1)} all-to-all(f32[128,1,128]{2,1,0:T(1,128)S(1)} %bitcast.17), channel_id=1, replica_groups=mesh['ens'=8,'rep'=16] {'ens','rep'}, dimensions={0} | all-to-all | bytes 131072 | tf_op jit(solution)/shard_map/all_to_all | solution.py:377
  25.3 0.0 copy-done
  25.3 0.0 copy-done.1
  25.3 0.0 copy-done.2
  25.3 0.0 copy-done.3
  25.3 0.0 copy-done.4
  25.3 0.0 copy-done.5
  25.3 4.6 %shard_map.122 = (f32[16,128]{1,0:T(8,128)}, bf16[2048,4096]{1,0:T(8,128)(2,1)S(1)}, bf16[512,2048]{1,0:T(8,128)(2,1)S(1)}, f32[512,256]{1,0:T(8,128)S(1)}) custom-call(s32[8,128]{1,0:T(8,128)S(4)} %get-tuple-element.22.table, bf16[256,4096]{1,0:T(8,128)(2,1)S(1)} %get-tuple-element.23.first_ref, bf16[2048,4096]{1,0:T(8,128)(2,1)} %states_ref.3, ...), custom_call_target="tpu_custom_call" | custom-call | flops 4294967296 | bytes 14680064 | tf_op jit(solution)/shard_map/pallas_call | solution.py:381
  29.9 1.0 %shard_map.123 = bf16[3,544,256]{2,1,0:T(8,128)(2,1)S(1)} custom-call(s32[8,128]{1,0:T(8,128)S(4)} %get-tuple-element.22.table, bf16[512,2048]{1,0:T(8,128)(2,1)S(1)} %get-tuple-element.27.d_hidden_ref, bf16[2048,4096]{1,0:T(8,128)(2,1)S(1)} %get-tuple-element.28.states_ref, f32[512,256]{1,0:T(8,128)S(1)} %get-tuple-element.29.grad_ref), custom_call_target="tpu_custom_call" | custom-call | flops 805306368 | bytes 786432 | tf_op jit(solution)/shard_map/pallas_call | solution.py:413
  30.9 0.1 collective-permute-start
  31.0 1.0 %shard_map.125 = bf16[3,544,256]{2,1,0:T(8,128)(2,1)S(1)} custom-call(s32[8,128]{1,0:T(8,128)S(4)} %get-tuple-element.22.table, bf16[512,2048]{1,0:T(8,128)(2,1)S(1)} %get-tuple-element.27.d_hidden_ref, bf16[2048,4096]{1,0:T(8,128)(2,1)S(1)} %get-tuple-element.28.states_ref, f32[512,256]{1,0:T(8,128)S(1)} %get-tuple-element.29.grad_ref), custom_call_target="tpu_custom_call" | custom-call | flops 805306368 | bytes 786432 | tf_op jit(solution)/shard_map/pallas_call | solution.py:413
  32.0 0.5 collective-permute-start.1
  32.5 0.7 shard_map.127
  33.2 0.3 collective-permute-start.4
  33.5 1.8 %collective-permute-done.4.rest_0_ = bf16[2,544,256]{2,1,0:T(8,128)(2,1)S(1)} collective-permute-done((bf16[2,544,256]{2,1,0:T(8,128)(2,1)S(1)}, bf16[2,544,256]{2,1,0:T(8,128)(2,1)S(1)}, u32[]{:S(2)}, u32[]{:S(2)}) %collective-permute-start.4) | collective-permute-done | bytes 557088 | tf_op jit(solution)/shard_map/ppermute | solution.py:40
  35.3 0.7 shard_map.128
  36.0 2.8 %collective-permute-start.5 = (bf16[544,256]{1,0:T(8,128)(2,1)S(1)}, bf16[544,256]{1,0:T(8,128)(2,1)S(1)}, u32[]{:S(2)}, u32[]{:S(2)}) collective-permute-start(bf16[544,256]{1,0:T(8,128)(2,1)S(1)} %get-tuple-element.34), channel_id=1, source_target_pairs={{0,2},{1,3},{2,4},{3,5},{4,6},{5,7},{6,0},{7,1},{8,10},{9,11},{10,... | collective-permute-start | bytes 835592 | tf_op jit(solution)/shard_map/ppermute | solution.py:40
  38.8 3.0 %collective-permute-start.6 = (bf16[544,256]{1,0:T(8,128)(2,1)S(1)}, bf16[544,256]{1,0:T(8,128)(2,1)S(1)}, u32[]{:S(2)}, u32[]{:S(2)}) collective-permute-start(bf16[544,256]{1,0:T(8,128)(2,1)S(1)} %get-tuple-element.35), channel_id=1, source_target_pairs={{0,6},{1,7},{2,0},{3,1},{4,2},{5,3},{6,4},{7,5},{8,14},{9,15},{10,... | collective-permute-start | bytes 835592 | tf_op jit(solution)/shard_map/ppermute | solution.py:40
  41.8 0.0 collective-permute-done.rest_0_
  41.8 1.1 %shard_map.124 = (f32[544,256]{1,0:T(8,128)S(1)}, f32[544,256]{1,0:T(8,128)S(1)}, f32[544,256]{1,0:T(8,128)S(1)}) custom-call(s32[8,128]{1,0:T(8,128)S(4)} %get-tuple-element.22.table, bf16[512,2048]{1,0:T(8,128)(2,1)S(1)} %get-tuple-element.27.d_hidden_ref, bf16[2048,4096]{1,0:T(8,128)(2,1)S(1)} %get-tuple-element.28.states_ref, ...), custom_call_target="tpu_custom_call" | custom-call | flops 805306368 | bytes 786432 | tf_op jit(solution)/shard_map/pallas_call | solution.py:413
  42.9 0.0 collective-permute-done.1.rest_0_
  42.9 0.9 %shard_map.126 = (bf16[544,256]{1,0:T(8,128)(2,1)S(1)}, bf16[544,256]{1,0:T(8,128)(2,1)S(1)}) custom-call(s32[8,128]{1,0:T(8,128)S(4)} %get-tuple-element.22.table, bf16[512,2048]{1,0:T(8,128)(2,1)S(1)} %get-tuple-element.27.d_hidden_ref, bf16[2048,4096]{1,0:T(8,128)(2,1)S(1)} %get-tuple-element.28.states_ref, f32[512,256]{1,0:T(8,128)S(1)} %get-tuple-element.29.grad_ref, ...), custom_call_target="tpu_custom_call" | custom-call | flops 536870912 | bytes 524288 | tf_op jit(solution)/shard_map/pallas_call | solution.py:413
  43.8 0.1 collective-permute-start.2
  43.9 3.2 %collective-permute-start.3 = (bf16[544,256]{1,0:T(8,128)(2,1)S(1)}, bf16[544,256]{1,0:T(8,128)(2,1)S(1)}, u32[]{:S(2)}, u32[]{:S(2)}) collective-permute-start(bf16[544,256]{1,0:T(8,128)(2,1)S(1)} %get-tuple-element.32), channel_id=1, source_target_pairs={{0,6},{1,7},{2,0},{3,1},{4,2},{5,3},{6,4},{7,5},{8,14},{9,15},{10,... | collective-permute-start | bytes 835592 | tf_op jit(solution)/shard_map/ppermute | solution.py:40
  47.1 0.4 shard_map.129
  47.5 6.5 %collective-permute-start.8 = (bf16[544,256]{1,0:T(8,128)(2,1)S(1)}, bf16[544,256]{1,0:T(8,128)(2,1)S(1)}, u32[]{:S(2)}, u32[]{:S(2)}) collective-permute-start(bf16[544,256]{1,0:T(8,128)(2,1)S(1)} %shard_map.129), channel_id=1, source_target_pairs={{0,8},{1,9},{2,10},{3,11},{4,12},{5,13},{6,14},{7,15},{8,0},{9,1},... | collective-permute-start | bytes 835592 | tf_op jit(solution)/shard_map/ppermute | solution.py:40
  54.0 0.0 collective-permute-done.5
  54.0 0.0 collective-permute-done.6
  54.0 0.1 add_convert_fusion.1
  54.1 0.8 %collective-permute-start.7 = (bf16[544,256]{1,0:T(8,128)(2,1)S(1)}, bf16[544,256]{1,0:T(8,128)(2,1)S(1)}, u32[]{:S(2)}, u32[]{:S(2)}) collective-permute-start(bf16[544,256]{1,0:T(8,128)(2,1)S(1)} %add_convert_fusion.1), channel_id=1, source_target_pairs={{0,8},{1,9},{2,10},{3,11},{4,12},{5,13},{6,14},{7,15},{8,0},{9,1},... | collective-permute-start | bytes 835592 | tf_op jit(solution)/shard_map/ppermute | solution.py:40
  54.9 6.6 %collective-permute-done.8 = bf16[544,256]{1,0:T(8,128)(2,1)S(1)} collective-permute-done((bf16[544,256]{1,0:T(8,128)(2,1)S(1)}, bf16[544,256]{1,0:T(8,128)(2,1)S(1)}, u32[]{:S(2)}, u32[]{:S(2)}) %collective-permute-start.8) | collective-permute-done | bytes 278560 | tf_op jit(solution)/shard_map/ppermute | solution.py:40
  61.5 0.1 add_convert_fusion
  61.6 1.0 %collective-permute-start.9 = (bf16[544,256]{1,0:T(8,128)(2,1)S(1)}, bf16[544,256]{1,0:T(8,128)(2,1)S(1)}, u32[]{:S(2)}, u32[]{:S(2)}) collective-permute-start(bf16[544,256]{1,0:T(8,128)(2,1)S(1)} %add_convert_fusion), channel_id=1, source_target_pairs={{0,4},{1,5},{2,6},{3,7},{4,0},{5,1},{6,2},{7,3},{8,12},{9,13},{10,... | collective-permute-start | bytes 835592 | tf_op jit(solution)/shard_map/ppermute | solution.py:40
  62.6 0.0 collective-permute-done.2
  62.6 0.0 collective-permute-done.3
  62.6 3.6 %collective-permute-done.7 = bf16[544,256]{1,0:T(8,128)(2,1)S(1)} collective-permute-done((bf16[544,256]{1,0:T(8,128)(2,1)S(1)}, bf16[544,256]{1,0:T(8,128)(2,1)S(1)}, u32[]{:S(2)}, u32[]{:S(2)}) %collective-permute-start.7) | collective-permute-done | bytes 278560 | tf_op jit(solution)/shard_map/ppermute | solution.py:40
  66.2 0.1 convert_add_fusion.own_ref
  66.3 3.4 %collective-permute-done.9.far_ref = bf16[544,256]{1,0:T(8,128)(2,1)S(1)} collective-permute-done((bf16[544,256]{1,0:T(8,128)(2,1)S(1)}, bf16[544,256]{1,0:T(8,128)(2,1)S(1)}, u32[]{:S(2)}, u32[]{:S(2)}) %collective-permute-start.9) | collective-permute-done | bytes 278560 | tf_op jit(solution)/shard_map/ppermute | solution.py:40
  69.7 1.0 %shard_map.130 = (f32[256,512]{1,0:T(8,128)}, f32[32,256]{1,0:T(8,128)}) custom-call(f32[544,256]{1,0:T(8,128)S(1)} %convert_add_fusion.own_ref, bf16[544,256]{1,0:T(8,128)(2,1)S(1)} %collective-permute-done.9.far_ref), custom_call_target="tpu_custom_call" | custom-call | bytes 1048576 | tf_op jit(solution)/shard_map/pallas_call | solution.py:445
Async XLA Ops:
  0.6 24.6 %copy-start = (bf16[1,512,256]{2,1,0:T(8,128)(2,1)S(1)}, bf16[1,512,256]{2,1,0:T(8,128)(2,1)}, u32[]{:S(2)}) copy-start(bf16[1,512,256]{2,1,0:T(8,128)(2,1)} %param.19) | copy-start | bytes 786436
  0.6 24.6 %copy-start.1 = (s32[16,16]{1,0:T(8,128)S(1)}, s32[16,16]{1,0:T(8,128)}, u32[]{:S(2)}) copy-start(s32[16,16]{1,0:T(8,128)} %table_ref.1) | copy-start | bytes 3076
  0.7 24.6 %copy-start.2 = (s32[2048]{0:T(1024)S(1)}, s32[2048]{0:T(1024)}, u32[]{:S(2)}) copy-start(s32[2048]{0:T(1024)} %param.14) | copy-start | bytes 24580
  0.7 24.6 %copy-start.3 = (f32[2048]{0:T(1024)S(1)}, f32[2048]{0:T(1024)}, u32[]{:S(2)}) copy-start(f32[2048]{0:T(1024)} %param.15) | copy-start | bytes 24580
  0.7 24.6 %copy-start.4 = (s32[2048]{0:T(1024)S(1)}, s32[2048]{0:T(1024)}, u32[]{:S(2)}) copy-start(s32[2048]{0:T(1024)} %param.16) | copy-start | bytes 24580
  0.7 24.6 %copy-start.5 = (f32[2048]{0:T(1024)S(1)}, f32[2048]{0:T(1024)}, u32[]{:S(2)}) copy-start(f32[2048]{0:T(1024)} %param.17) | copy-start | bytes 24580
  30.9 10.9 %collective-permute-start = (bf16[3,544,256]{2,1,0:T(8,128)(2,1)S(1)}, bf16[3,544,256]{2,1,0:T(8,128)(2,1)S(1)}, u32[]{:S(2)}, u32[]{:S(2)}) collective-permute-start(bf16[3,544,256]{2,1,0:T(8,128)(2,1)S(1)} %shard_map.123), channel_id=1, source_target_pairs={{0,1},{1,0},{2,3},{3,2},{4,5},{5,4},{6,7},{7,6},{8,9},{9,8},{10,11... | collective-permute-start | bytes 2506760 | tf_op jit(solution)/shard_map/ppermute | solution.py:40
  32.0 10.9 %collective-permute-start.1 = (bf16[3,544,256]{2,1,0:T(8,128)(2,1)S(1)}, bf16[3,544,256]{2,1,0:T(8,128)(2,1)S(1)}, u32[]{:S(2)}, u32[]{:S(2)}) collective-permute-start(bf16[3,544,256]{2,1,0:T(8,128)(2,1)S(1)} %shard_map.125), channel_id=1, source_target_pairs={{0,1},{1,0},{2,3},{3,2},{4,5},{5,4},{6,7},{7,6},{8,9},{9,8},{10,11... | collective-permute-start | bytes 2506760 | tf_op jit(solution)/shard_map/ppermute | solution.py:40
  33.2 2.1 %collective-permute-start.4 = (bf16[2,544,256]{2,1,0:T(8,128)(2,1)S(1)}, bf16[2,544,256]{2,1,0:T(8,128)(2,1)S(1)}, u32[]{:S(2)}, u32[]{:S(2)}) collective-permute-start(bf16[2,544,256]{2,1,0:T(8,128)(2,1)S(1)} %shard_map.127), channel_id=1, source_target_pairs={{0,1},{1,0},{2,3},{3,2},{4,5},{5,4},{6,7},{7,6},{8,9},{9,8},{10,11... | collective-permute-start | bytes 1671176 | tf_op jit(solution)/shard_map/ppermute | solution.py:40
  36.0 18.0 %collective-permute-start.5 = (bf16[544,256]{1,0:T(8,128)(2,1)S(1)}, bf16[544,256]{1,0:T(8,128)(2,1)S(1)}, u32[]{:S(2)}, u32[]{:S(2)}) collective-permute-start(bf16[544,256]{1,0:T(8,128)(2,1)S(1)} %get-tuple-element.34), channel_id=1, source_target_pairs={{0,2},{1,3},{2,4},{3,5},{4,6},{5,7},{6,0},{7,1},{8,10},{9,11},{10,... | collective-permute-start | bytes 835592 | tf_op jit(solution)/shard_map/ppermute | solution.py:40
  38.8 15.2 %collective-permute-start.6 = (bf16[544,256]{1,0:T(8,128)(2,1)S(1)}, bf16[544,256]{1,0:T(8,128)(2,1)S(1)}, u32[]{:S(2)}, u32[]{:S(2)}) collective-permute-start(bf16[544,256]{1,0:T(8,128)(2,1)S(1)} %get-tuple-element.35), channel_id=1, source_target_pairs={{0,6},{1,7},{2,0},{3,1},{4,2},{5,3},{6,4},{7,5},{8,14},{9,15},{10,... | collective-permute-start | bytes 835592 | tf_op jit(solution)/shard_map/ppermute | solution.py:40
  43.8 18.7 %collective-permute-start.2 = (bf16[544,256]{1,0:T(8,128)(2,1)S(1)}, bf16[544,256]{1,0:T(8,128)(2,1)S(1)}, u32[]{:S(2)}, u32[]{:S(2)}) collective-permute-start(bf16[544,256]{1,0:T(8,128)(2,1)S(1)} %get-tuple-element.31), channel_id=1, source_target_pairs={{0,2},{1,3},{2,4},{3,5},{4,6},{5,7},{6,0},{7,1},{8,10},{9,11},{10,... | collective-permute-start | bytes 835592 | tf_op jit(solution)/shard_map/ppermute | solution.py:40
  43.9 18.7 %collective-permute-start.3 = (bf16[544,256]{1,0:T(8,128)(2,1)S(1)}, bf16[544,256]{1,0:T(8,128)(2,1)S(1)}, u32[]{:S(2)}, u32[]{:S(2)}) collective-permute-start(bf16[544,256]{1,0:T(8,128)(2,1)S(1)} %get-tuple-element.32), channel_id=1, source_target_pairs={{0,6},{1,7},{2,0},{3,1},{4,2},{5,3},{6,4},{7,5},{8,14},{9,15},{10,... | collective-permute-start | bytes 835592 | tf_op jit(solution)/shard_map/ppermute | solution.py:40
  47.5 14.0 %collective-permute-start.8 = (bf16[544,256]{1,0:T(8,128)(2,1)S(1)}, bf16[544,256]{1,0:T(8,128)(2,1)S(1)}, u32[]{:S(2)}, u32[]{:S(2)}) collective-permute-start(bf16[544,256]{1,0:T(8,128)(2,1)S(1)} %shard_map.129), channel_id=1, source_target_pairs={{0,8},{1,9},{2,10},{3,11},{4,12},{5,13},{6,14},{7,15},{8,0},{9,1},... | collective-permute-start | bytes 835592 | tf_op jit(solution)/shard_map/ppermute | solution.py:40
  54.1 12.1 %collective-permute-start.7 = (bf16[544,256]{1,0:T(8,128)(2,1)S(1)}, bf16[544,256]{1,0:T(8,128)(2,1)S(1)}, u32[]{:S(2)}, u32[]{:S(2)}) collective-permute-start(bf16[544,256]{1,0:T(8,128)(2,1)S(1)} %add_convert_fusion.1), channel_id=1, source_target_pairs={{0,8},{1,9},{2,10},{3,11},{4,12},{5,13},{6,14},{7,15},{8,0},{9,1},... | collective-permute-start | bytes 835592 | tf_op jit(solution)/shard_map/ppermute | solution.py:40
  61.6 8.1 %collective-permute-start.9 = (bf16[544,256]{1,0:T(8,128)(2,1)S(1)}, bf16[544,256]{1,0:T(8,128)(2,1)S(1)}, u32[]{:S(2)}, u32[]{:S(2)}) collective-permute-start(bf16[544,256]{1,0:T(8,128)(2,1)S(1)} %add_convert_fusion), channel_id=1, source_target_pairs={{0,4},{1,5},{2,6},{3,7},{4,0},{5,1},{6,2},{7,3},{8,12},{9,13},{10,... | collective-permute-start | bytes 835592 | tf_op jit(solution)/shard_map/ppermute | solution.py:40
